TPU v7x, 32 devices: a whole 2x2x4 slice. The times are simulated.
32 devices in a mesh: row: 4 (over x, core), col: 8 (over z, y).
Axes of the slice: x: 2, y: 2, z: 4, core: 2. Of those that a mesh axis runs over, the one named last changes fastest.
Arguments:
- markov: bfloat16 [2, 256, 128, 128], P(None, 'col'), may hold values from -6 to 6
- omega: bfloat16 [32768, 64], P('col'), may hold values from -0.03125 to 0.03125
Outputs:
- denoised: float32 [2, 256, 128, 128], P(None, 'col')
All inputs are finite; a program needn't handle non-finite values.
Results may differ from a plain program's by a relative error of at most 0.0007.
Values may be sent and summed in bfloat16 or wider, within the bound.
No kernel may reach another device: no remote copies, remote signals or barrier semaphores. Data moves between devices by JAX's collectives and lax.ppermute only.
A program may use at most 64 MiB of HBM per device.

v0:
```python
import jax
import jax.numpy as jnp
from jax import lax
from jax.sharding import PartitionSpec as P

NS_STEPS = 8


norm_floor = 1e-06
highest = lax.Precision.HIGHEST


def shifted(block, axis, distance):
    devices = range(lax.axis_size(axis))
    route = [((i - distance) % len(devices), i) for i in devices]
    return lax.ppermute(block, axis, route)


def column_gram(matrix):
    return lax.dot_general(
        matrix,
        matrix,
        (((0,), (0,)), ((), ())),
        precision=highest,
        preferred_element_type=jnp.float32,
    )


def square_mul(left, right):
    return jnp.dot(left, right, precision=highest, preferred_element_type=jnp.float32)


def total_gram(partial_value):
    return lax.psum(partial_value, "row")


def orthonormal(sketch):
    gram = total_gram(column_gram(sketch))
    scale = 1.0 / jnp.sqrt(jnp.trace(gram) + norm_floor)
    coeffs = jnp.eye(gram.shape[0], dtype=jnp.float32) * scale
    for sweep in range(NS_STEPS):
        inner = square_mul(square_mul(coeffs.T, gram), coeffs)
        coeffs = 1.5 * coeffs - 0.5 * square_mul(coeffs, inner)
    return square_mul(sketch, coeffs)


def pick_half(pair, half_id):
    return jnp.where(half_id == 0, pair[0], pair[1])


def lag_sums(basis_blocks, column_rows, column_count):
    row_count, out_rows, rank_extent = basis_blocks.shape
    input_columns = column_rows.shape[1] // column_count
    start_total = jnp.zeros((out_rows, row_count + column_count, input_columns), jnp.float32)

    def add_row(row_position, running):
        orthonormal_row_vector = lax.dynamic_index_in_dim(
            basis_blocks, row_position, 0, keepdims=False
        )
        product = jnp.dot(orthonormal_row_vector, column_rows, preferred_element_type=jnp.float32)
        product = product.reshape(out_rows, column_count, input_columns)
        current_sum = lax.dynamic_slice_in_dim(running, row_position, column_count, 1)
        return lax.dynamic_update_slice_in_dim(running, current_sum + product, row_position, 1)

    return lax.fori_loop(0, row_count, add_row, start_total)


def local(markov, omega):
    n_rows = lax.axis_size("row")
    n_cols = lax.axis_size("col")
    row_position = lax.axis_index("row")
    col_id = lax.axis_index("col")
    halves, blocks, out_rows, input_columns = markov.shape
    rank_extent = omega.shape[1]
    bit_count = (n_rows - 1).bit_length()
    held = markov
    for bit_pos in range(bit_count):
        moved = shifted(held, "col", -(1 << bit_pos))
        held = jnp.where(row_position // (1 << bit_pos) % 2 == 1, moved, held)
    following = shifted(held, "col", -1)
    first_block = row_position + col_id
    window = jnp.concatenate(
        [pick_half(held, first_block // n_cols), pick_half(following, (first_block + 1) // n_cols)],
        axis=0,
    )
    omega_blocks = omega.reshape(blocks, input_columns, rank_extent)

    def slab_at(column_id):
        return lax.dynamic_slice_in_dim(window, column_id, blocks, 0).reshape(
            blocks * out_rows, input_columns
        )

    def range_step(column_id, running):
        weights = lax.dynamic_index_in_dim(omega_blocks, column_id, 0, keepdims=False)
        return running + jnp.dot(slab_at(column_id), weights, preferred_element_type=jnp.float32)

    partial_value = lax.fori_loop(
        0, blocks, range_step, jnp.zeros((blocks * out_rows, rank_extent), jnp.float32)
    )
    sketch = lax.psum(partial_value, "col")
    basis = orthonormal(sketch).astype(jnp.bfloat16)

    def projection_update(column_id, running):
        term = lax.dot_general(
            basis, slab_at(column_id), (((0,), (0,)), ((), ())), preferred_element_type=jnp.float32
        )
        return lax.dynamic_update_slice_in_dim(running, term, column_id * input_columns, 1)

    projected_matrix = lax.fori_loop(
        0, blocks, projection_update, jnp.zeros((rank_extent, blocks * input_columns), jnp.float32)
    )
    projected_matrix = lax.psum(projected_matrix, "row").astype(jnp.bfloat16)
    basis_blocks = basis.reshape(blocks, out_rows, rank_extent)
    local_sums = lag_sums(basis_blocks, projected_matrix, blocks).transpose(1, 0, 2)
    for bit_pos in range(bit_count):
        moved = shifted(local_sums.astype(jnp.bfloat16), "col", 1 << bit_pos).astype(
            local_sums.dtype
        )
        local_sums = jnp.where(row_position // (1 << bit_pos) % 2 == 1, moved, local_sums)
    carried = shifted(local_sums[blocks:].astype(jnp.bfloat16), "col", 1).astype(jnp.float32)
    own_half = (col_id < row_position).astype(jnp.int32)
    prev_col = (col_id + n_cols - 1) % n_cols
    carry_half = (prev_col + n_cols * (prev_col < row_position).astype(jnp.int32) + 1) // n_cols
    owned = jnp.stack(
        [
            jnp.where(own_half == half_id, local_sums[:blocks], 0.0)
            + jnp.where(carry_half == half_id, carried, 0.0)
            for half_id in range(2)
        ]
    )
    totals = lax.psum(owned, "row")
    total_rows = blocks * n_rows
    total_cols = blocks * n_cols
    lag_ids = (
        jnp.arange(2, dtype=jnp.int32)[:, None] * total_cols
        + col_id * blocks
        + jnp.arange(blocks, dtype=jnp.int32)[None, :]
    )
    counts = jnp.maximum(
        jnp.minimum(lag_ids, total_rows - 1) - jnp.maximum(0, lag_ids - total_cols + 1) + 1, 0
    )
    counts_f = counts.astype(jnp.float32)[:, :, None, None]
    measured = markov.astype(jnp.float32)
    averaged = totals / jnp.maximum(counts_f, 1.0)
    return jnp.where(counts_f > 0, 0.5 * measured + 0.5 * averaged, measured)


def solution(mesh):
    in_specs = (P(None, "col", None, None), P("col", None))
    out_specs = P(None, "col", None, None)
    return jax.shard_map(local, mesh=mesh, in_specs=in_specs, out_specs=out_specs, check_vma=False)
```

profile of v0, /device:TPU:0, one launch (start us, length us, event | category | flops | bytes accessed | tf_op | source)
XLA Modules:
  0.0 767.1 jit_solution(6744331033921523730)
XLA Ops:
  6.5 6.0 collective-permute-start
  12.6 45.2 %collective-permute-done = bf16[2,32,128,128]{3,2,1,0:T(8,128)(2,1)} collective-permute-done((bf16[2,32,128,128]{3,2,1,0:T(8,128)(2,1)}, bf16[2,32,128,128]{3,2,1,0:T(8,128)(2,1)}, u32[]{:S(2)}, u32[]{:S(2)}) %collective-permute-start) | collective-permute-done | bytes 2097184 | tf_op jit(solution)/shard_map/ppermute | solution.py:16
  61.2 45.1 %collective-permute-done.1 = bf16[2,32,128,128]{3,2,1,0:T(8,128)(2,1)} collective-permute-done((bf16[2,32,128,128]{3,2,1,0:T(8,128)(2,1)S(1)}, bf16[2,32,128,128]{3,2,1,0:T(8,128)(2,1)}, u32[]{:S(2)}, u32[]{:S(2)}) %collective-permute-start.1) | collective-permute-done | bytes 2097184 | tf_op jit(solution)/shard_map/ppermute | solution.py:16
  107.8 7.0 collective-permute-start.2
  117.8 40.5 %collective-permute-done.2 = bf16[2,32,128,128]{3,2,1,0:T(8,128)(2,1)S(1)} collective-permute-done((bf16[2,32,128,128]{3,2,1,0:T(8,128)(2,1)}, bf16[2,32,128,128]{3,2,1,0:T(8,128)(2,1)S(1)}, u32[]{:S(2)}, u32[]{:S(2)}) %collective-permute-start.2) | collective-permute-done | bytes 2097184 | tf_op jit(solution)/shard_map/ppermute | solution.py:16
  158.6 92.9 %while.42 = (s32[]{:T(128)}, f32[4096,64]{0,1:T(8,128)}, bf16[64,128,128]{2,1,0:T(8,128)(2,1)S(1)}, bf16[32,128,64]{2,1,0:T(8,128)(2,1)}, s32[]{:T(128)}, /*index=5*/s32[]{:T(128)}) while((s32[]{:T(128)}, f32[4096,64]{0,1:T(8,128)}, bf16[64,128,128]{2,1,0:T(8,128)(2,1)S(1)}, bf16[32,128,64]{2,1,0:T(8,128)(2,1)}, s32[]{:T(128)}, ...), condition=%wide.region_1.2_spmd.clone, body=%wide.region_0.1_spmd.clone.sunk | while | flops 67633152 | bytes 5276243 | solution.py:97
  251.6 81.7 %all-reduce.4.cloned.1.call-done = f32[4096,64]{0,1:T(8,128)} async-done(((f32[4096,64]{0,1:T(8,128)}), f32[4096,64]{0,1:T(8,128)}) %all-reduce.4.cloned.1.call-update) | async-done | bytes 1048592 | tf_op jit(solution)/shard_map/psum | solution.py:100
  335.9 11.3 %psum.29 = f32[64,64]{1,0:T(8,128)S(1)} all-reduce(f32[64,64]{1,0:T(8,128)S(1)} %fusion.39), channel_id=1, replica_groups=mesh['row'=4,'col'=8] {'row'}, use_global_device_ids=true, to_apply=%region_3.4 | all-reduce | flops 4096 | bytes 32768 | tf_op jit(solution)/shard_map/psum | solution.py:34
  359.6 39.2 %while.40 = (s32[]{:T(128)}, f32[64,4096]{1,0:T(8,128)}, bf16[64,128,128]{2,1,0:T(8,128)(2,1)S(1)}, bf16[4096,64]{1,0:T(8,128)(2,1)S(1)}, s32[]{:T(128)}, /*index=5*/s32[]{:T(128)}, s32[]{:T(128)}, s32[]{:T(128)}) while((s32[]{:T(128)}, f32[64,4096]{1,0:T(8,128)}, bf16[64,128,128]{2,1,0:T(8,128)(2,1)S(1)}, bf16[4096,64]{1,0:T(8,128)(2,1)S(1)}, ...), condition=%wide.region_6.7_spmd, body=%wide.region_5.6_spmd.sunk | while | flops 67108872 | bytes 3702923 | solution.py:109
  398.9 26.3 %all-reduce.7 = bf16[64,4096]{1,0:T(8,128)(2,1)S(1)} all-reduce(f32[64,4096]{1,0:T(8,128)} %get-tuple-element.243), channel_id=1, replica_groups=mesh['row'=4,'col'=8] {'row'}, use_global_device_ids=true, to_apply=%region_7.8 | all-reduce | flops 262144 | bytes 1572864 | tf_op jit(solution)/shard_map/psum | solution.py:112
  427.7 108.3 %while.41 = (s32[]{:T(128)}, f32[128,64,128]{2,0,1:T(8,128)}, bf16[32,128,64]{1,2,0:T(8,128)(2,1)}, bf16[64,4096]{1,0:T(8,128)(2,1)S(1)}, s32[]{:T(128)}) while((s32[]{:T(128)}, f32[128,64,128]{2,0,1:T(8,128)}, bf16[32,128,64]{1,2,0:T(8,128)(2,1)}, bf16[64,4096]{1,0:T(8,128)(2,1)S(1)}, s32[]{:T(128)}) %tuple.87), condition=%wide.region_9.10_spmd, body=%wide.region_8.9_spmd.sunk | while | flops 67633152 | bytes 4736061 | solution.py:65
  434.5 3.4 add_dynamic-update-slice_fusion.2
  437.9 3.4 add_dynamic-update-slice_fusion.2
  444.7 3.4 add_dynamic-update-slice_fusion.2
  448.0 3.4 add_dynamic-update-slice_fusion.2
  451.4 3.4 add_dynamic-update-slice_fusion.2
  454.8 3.4 add_dynamic-update-slice_fusion.2
  458.2 3.4 add_dynamic-update-slice_fusion.2
  461.6 3.4 add_dynamic-update-slice_fusion.2
  539.3 50.2 %collective-permute-done.3 = bf16[64,128,128]{2,1,0:T(8,128)(2,1)S(1)} collective-permute-done((bf16[64,128,128]{2,1,0:T(8,128)(2,1)S(1)}, bf16[64,128,128]{2,1,0:T(8,128)(2,1)S(1)}, u32[]{:S(2)}, u32[]{:S(2)}) %collective-permute-start.3) | collective-permute-done | bytes 2097184 | tf_op jit(solution)/shard_map/ppermute | solution.py:16
  590.2 48.9 %collective-permute-done.4 = bf16[64,128,128]{2,1,0:T(8,128)(2,1)S(1)} collective-permute-done((bf16[64,128,128]{2,1,0:T(8,128)(2,1)S(1)}, bf16[64,128,128]{2,1,0:T(8,128)(2,1)S(1)}, u32[]{:S(2)}, u32[]{:S(2)}) %collective-permute-start.4) | collective-permute-done | bytes 2097184 | tf_op jit(solution)/shard_map/ppermute | solution.py:16
  642.6 26.4 %collective-permute-done.5 = bf16[32,128,128]{2,1,0:T(8,128)(2,1)S(1)} collective-permute-done((bf16[32,128,128]{2,1,0:T(8,128)(2,1)S(1)}, bf16[32,128,128]{2,1,0:T(8,128)(2,1)S(1)}, u32[]{:S(2)}, u32[]{:S(2)}) %collective-permute-start.5) | collective-permute-done | bytes 1048608 | tf_op jit(solution)/shard_map/ppermute | solution.py:16
  673.6 81.6 %all-reduce.6.cloned.1.call-done = f32[2,32,128,128]{3,2,1,0:T(8,128)} async-done(((f32[2,32,128,128]{3,2,1,0:T(8,128)}), f32[2,32,128,128]{3,2,1,0:T(8,128)}) %all-reduce.6.cloned.1.call-update) | async-done | bytes 4194320 | tf_op jit(solution)/shard_map/psum | solution.py:131
  755.3 5.0 convert_select_fusion
  (217 shorter events, 249.5 us)
Async XLA Ops:
  6.5 326.8 %all-reduce.4.cloned.1.call-start = ((), (), s32[]{:S(2)}) async-start(), calls=%async_computation | async-start | bytes 2097152 | tf_op jit(solution)/shard_map/psum | solution.py:100
  6.5 51.2 %collective-permute-start = (bf16[2,32,128,128]{3,2,1,0:T(8,128)(2,1)}, bf16[2,32,128,128]{3,2,1,0:T(8,128)(2,1)}, u32[]{:S(2)}, u32[]{:S(2)}) collective-permute-start(bf16[2,32,128,128]{3,2,1,0:T(8,128)(2,1)} %param.8), channel_id=1, source_target_pairs={{1,0},{2,1},{3,2},{4,3},{5,4},{6,5},{7,6},{0,7},{9,8},{10,9},{11,1... | collective-permute-start | bytes 6291464 | tf_op jit(solution)/shard_map/ppermute | solution.py:16
  59.6 46.7 %collective-permute-start.1 = (bf16[2,32,128,128]{3,2,1,0:T(8,128)(2,1)S(1)}, bf16[2,32,128,128]{3,2,1,0:T(8,128)(2,1)}, u32[]{:S(2)}, u32[]{:S(2)}) collective-permute-start(bf16[2,32,128,128]{3,2,1,0:T(8,128)(2,1)S(1)} %broadcast_select_fusion), channel_id=1, source_target_pairs={{2,0},{3,1},{4,2},{5,3},{6,4},{7,5},{0,6},{1,7},{10,8},{11,9},{12,... | collective-permute-start | bytes 6291464 | tf_op jit(solution)/shard_map/ppermute | solution.py:16
  61.2 53.6 %copy-start.4 = (bf16[4096,64]{0,1:T(8,128)(2,1)S(1)}, bf16[4096,64]{0,1:T(8,128)(2,1)}, u32[]{:S(2)}) copy-start(bf16[4096,64]{0,1:T(8,128)(2,1)} %param.9) | copy-start | bytes 1572868
  107.8 50.5 %collective-permute-start.2 = (bf16[2,32,128,128]{3,2,1,0:T(8,128)(2,1)}, bf16[2,32,128,128]{3,2,1,0:T(8,128)(2,1)S(1)}, u32[]{:S(2)}, u32[]{:S(2)}) collective-permute-start(bf16[2,32,128,128]{3,2,1,0:T(8,128)(2,1)} %broadcast_select_fusion.1), channel_id=1, source_target_pairs={{1,0},{2,1},{3,2},{4,3},{5,4},{6,5},{7,6},{0,7},{9,8},{10,9},{11,1... | collective-permute-start | bytes 6291464 | tf_op jit(solution)/shard_map/ppermute | solution.py:16
  251.5 503.7 %all-reduce.6.cloned.1.call-start = ((), (), s32[]{:S(2)}) async-start(), calls=%async_computation.1 | async-start | bytes 8388608 | tf_op jit(solution)/shard_map/psum | solution.py:131
  333.3 19.9 %copy-start.2 = (f32[4096,64]{0,1:T(8,128)S(1)}, f32[4096,64]{0,1:T(8,128)}, u32[]{:S(2)}) copy-start(f32[4096,64]{0,1:T(8,128)} %all-reduce.4.cloned.1.call-done) | copy-start | bytes 3145732
  536.1 53.4 %copy-start = (f32[128,64,128]{2,0,1:T(8,128)S(1)}, f32[128,64,128]{2,0,1:T(8,128)}, u32[]{:S(2)}) copy-start(f32[128,64,128]{2,0,1:T(8,128)} %get-tuple-element.244) | copy-start | bytes 12582916
  538.8 50.7 %collective-permute-start.3 = (bf16[64,128,128]{2,1,0:T(8,128)(2,1)S(1)}, bf16[64,128,128]{2,1,0:T(8,128)(2,1)S(1)}, u32[]{:S(2)}, u32[]{:S(2)}) collective-permute-start(bf16[64,128,128]{2,1,0:T(8,128)(2,1)S(1)} %bitcast_convert_fusion), channel_id=1, source_target_pairs={{7,0},{0,1},{1,2},{2,3},{3,4},{4,5},{5,6},{6,7},{15,8},{8,9},{9,10... | collective-permute-start | bytes 6291464 | tf_op jit(solution)/shard_map/ppermute | solution.py:16
  590.1 48.9 %collective-permute-start.4 = (bf16[64,128,128]{2,1,0:T(8,128)(2,1)S(1)}, bf16[64,128,128]{2,1,0:T(8,128)(2,1)S(1)}, u32[]{:S(2)}, u32[]{:S(2)}) collective-permute-start(bf16[64,128,128]{2,1,0:T(8,128)(2,1)S(1)} %fusion.10), channel_id=1, source_target_pairs={{6,0},{7,1},{0,2},{1,3},{2,4},{3,5},{4,6},{5,7},{14,8},{15,9},{8,1... | collective-permute-start | bytes 6291464 | tf_op jit(solution)/shard_map/ppermute | solution.py:16
  640.3 2.0 copy-start.1
  642.4 26.5 %collective-permute-start.5 = (bf16[32,128,128]{2,1,0:T(8,128)(2,1)S(1)}, bf16[32,128,128]{2,1,0:T(8,128)(2,1)S(1)}, u32[]{:S(2)}, u32[]{:S(2)}) collective-permute-start(bf16[32,128,128]{2,1,0:T(8,128)(2,1)S(1)} %slice.43), channel_id=1, source_target_pairs={{7,0},{0,1},{1,2},{2,3},{3,4},{4,5},{5,6},{6,7},{15,8},{8,9},{9,10... | collective-permute-start | bytes 3145736 | tf_op jit(solution)/shard_map/ppermute | solution.py:16
  673.5 81.8 %copy-start.3 = (bf16[2,32,128,128]{3,2,1,0:T(8,128)(2,1)S(1)}, bf16[2,32,128,128]{3,2,1,0:T(8,128)(2,1)}, u32[]{:S(2)}) copy-start(bf16[2,32,128,128]{3,2,1,0:T(8,128)(2,1)} %param.8) | copy-start | bytes 6291460
Sparse Core Ops, SparseCore 0:
  251.7 81.5 all-reduce.3
  673.6 81.6 all-reduce.5
where the time goes:
time: 770 us; the launch traced here: 767 us
  waiting for transfers between devices  420 us (55%)
  matrix products  242 us (31%)
  blocking collectives  37.7 us (5%)
  other arithmetic  20.1 us (3%)
  local copies, waits for them, and re-layouts  17 us (2%)
  starting transfers between devices  15.3 us (2%)
  between operations  14.5 us (2%)
    ppermute x6, waiting for transfers between devices, shifted(): return lax.ppermute(block, axis, route)  256 us
    dot_general x32, matrix products, add_row(): jnp.dot(orthonormal_row_vector, column_rows, preferred_element_type=jnp.f...  108 us
    dot_general x32, matrix products, range_step(): jnp.dot(slab_at(column_id), weights, preferred_element_type=jnp.float32)  89.3 us
    psum x1, waiting for transfers between devices, local(): sketch = lax.psum(partial_value, 'col')  81.7 us
    psum x1, waiting for transfers between devices, local(): totals = lax.psum(owned, 'row')  81.6 us
    dot_general x32, matrix products, projection_update(): lax.dot_general(basis, slab_at(column_id), (((0,), (0,)), ((), ())), pref...  35.7 us
    psum x1, blocking collectives, local(): projected_matrix = lax.psum(projected_matrix, 'row').astype(jnp.bfloat16)  26.3 us
  transfers between devices with their start and end apart: 8, of which 8 were waited for; matrix products, arithmetic and copies ran while one was open for 0% of the time, Pallas kernels for 0%

commit v1 on v0

v1 whole, which is shorter than its diff:
```python
import functools

import jax
import jax.numpy as jnp
from jax import lax
from jax.experimental import pallas as pl
from jax.experimental.pallas import tpu as pltpu
from jax.sharding import PartitionSpec as P

NS_STEPS = 8
norm_floor = 1e-06
SHARE = 0.375
F32 = jnp.float32
BF16 = jnp.bfloat16
HIGHEST = lax.Precision.HIGHEST
VMEM_LIMIT = 56 * 1024 * 1024

NT = (((1,), (1,)), ((), ()))
NN = (((1,), (0,)), ((), ()))


def matmul(left, right, dims=NN):
    return lax.dot_general(left, right, dims, preferred_element_type=F32)


def shift_col(x, distance):
    n = lax.axis_size("col")
    return lax.ppermute(x, "col", [(i, (i + distance) % n) for i in range(n)])


def swap_row(x, bit):
    n = lax.axis_size("row")
    return lax.ppermute(x, "row", [(i, i ^ bit) for i in range(n)])


def gather_row(x):
    pieces, offsets = [x], [0]
    bit = lax.axis_size("row") // 2
    while bit:
        pieces = pieces + [swap_row(p, bit) for p in pieces]
        offsets = offsets + [o ^ bit for o in offsets]
        bit //= 2
    return pieces, offsets


def sketch_kernel(count, half_ref, lag_ref, *refs):
    w_refs, out_ref, lags, acc, sems = refs[:count], refs[count], refs[count + 1], refs[count + 2], refs[count + 3]
    blocks = lag_ref.shape[1]
    pairs, kk, _ = w_refs[0].shape
    rows = out_ref.shape[0]
    copies = [
        pltpu.make_async_copy(lag_ref.at[h], lags.at[h, pl.ds(1, blocks)], sems.at[h]) for h in range(2)
    ]
    for copy in copies:
        copy.start()
    zero = jnp.zeros(lags.shape[2:], BF16)
    for h in range(2):
        lags[h, 0] = zero
        lags[h, blocks + 1] = zero
        lags[h, blocks + 2] = zero
    acc[...] = jnp.zeros_like(acc)
    for copy in copies:
        copy.wait()

    def step(t, carry):
        for e in range(count):
            h = half_ref[e]
            before, here, after = lags[h, 2 * t], lags[h, 2 * t + 1], lags[h, 2 * t + 2]
            tile = jnp.concatenate(
                [jnp.concatenate([before, here], 1), jnp.concatenate([here, after], 1)], 0
            )
            part = matmul(w_refs[e][...].reshape(pairs * kk, 256), tile, NT)
            acc[pl.ds(pairs * (e + 1) - t, pairs)] += part.reshape(pairs, kk, 256)
        return carry

    lax.fori_loop(0, pairs + 1, step, 0)

    def store(q, carry):
        out_ref[2 * q] = acc[q + pairs, :, :128].astype(BF16)
        out_ref[2 * q + 1] = acc[q + pairs + 1, :, 128:].astype(BF16)
        return carry

    lax.fori_loop(0, rows // 2, store, 0)


def sketch_part(halves, markov, w_blocks, rows):
    count = len(w_blocks)
    blocks = markov.shape[1]
    pairs, kk, _ = w_blocks[0].shape
    return pl.pallas_call(
        functools.partial(sketch_kernel, count),
        out_shape=jax.ShapeDtypeStruct((rows, kk, 128), BF16),
        in_specs=[pl.BlockSpec(memory_space=pltpu.SMEM), pl.BlockSpec(memory_space=pl.ANY)]
        + [pl.BlockSpec(memory_space=pltpu.VMEM)] * count,
        out_specs=pl.BlockSpec(memory_space=pltpu.VMEM),
        scratch_shapes=[
            pltpu.VMEM((2, blocks + 3, 128, 128), BF16),
            pltpu.VMEM((pairs * (count + 1), kk, 256), F32),
            pltpu.SemaphoreType.DMA((2,)),
        ],
        compiler_params=pltpu.CompilerParams(vmem_limit_bytes=VMEM_LIMIT),
        name="sketch",
    )(halves, markov, *w_blocks)


def split(x):
    high = x.astype(BF16)
    return high, (x - high.astype(F32)).astype(BF16)


def full_dot(left, right):
    return jnp.dot(left, right, precision=HIGHEST, preferred_element_type=F32)


def newton_schulz(gram):
    size = gram.shape[0]
    row = lax.broadcasted_iota(jnp.int32, (size, size), 0)
    col = lax.broadcasted_iota(jnp.int32, (size, size), 1)
    eye = jnp.where(row == col, 1.0, 0.0)
    scale = 1.0 / jnp.sqrt(jnp.sum(gram * eye, keepdims=True) + norm_floor)
    inner = gram * (scale * scale)
    coeffs = eye * scale
    for sweep in range(NS_STEPS):
        update = 1.5 * eye - 0.5 * inner
        coeffs = full_dot(coeffs, update)
        if sweep + 1 < NS_STEPS:
            inner = full_dot(full_dot(inner, update), update)
    return coeffs


def needed(half_ref, count, pairs, h, g):
    first = (2 * g) // pairs
    second = jnp.minimum(first + 1, count - 1)
    return jnp.logical_or(half_ref[first] == h, half_ref[second] == h)


def basis_tile(basis_ref, g, rank):
    step = 256 // rank
    low = pl.multiple_of(g * (step * rank), 64)
    return jnp.concatenate(
        [basis_ref[pl.ds(low + rank, 256), :], basis_ref[pl.ds(low, 256), :]], 1
    )


def project_kernel(count, pieces, half_ref, *refs):
    s_refs = refs[:pieces]
    lt_ref, basis_ref, out_ref, sketch, acc = refs[pieces:]
    rows, kk, _ = s_refs[0].shape
    rank = kk * pieces
    group = 256 // rank
    _, pairs, mm, _ = out_ref.shape
    groups = rows // group

    def load(g, gram):
        block = jnp.concatenate(
            [s_refs[j][group * g + i] for i in range(group) for j in range(pieces)], 0
        )
        sketch[pl.ds(pl.multiple_of(g * 256, 256), 256), :] = block
        return gram + matmul(block, block, NT)

    gram4 = lax.fori_loop(0, groups, load, jnp.zeros((256, 256), F32))
    gram = sum(
        gram4[rank * i : rank * (i + 1), rank * i : rank * (i + 1)] for i in range(group)
    )
    coeffs = newton_schulz(gram)
    wide = jnp.concatenate([coeffs] * group, 1)
    wide = jnp.concatenate([wide] * group, 0)
    row = lax.broadcasted_iota(jnp.int32, (256, 256), 0) // rank
    col = lax.broadcasted_iota(jnp.int32, (256, 256), 1) // rank
    wide = jnp.where(row == col, wide, 0.0)
    high, low = split(wide)

    basis_ref[pl.ds(0, 2 * rank), :] = jnp.zeros((2 * rank, 128), BF16)
    basis_ref[pl.ds((rows + 2) * rank, 3 * rank), :] = jnp.zeros((3 * rank, 128), BF16)

    def rotate(g, carry):
        block = sketch[pl.ds(pl.multiple_of(g * 256, 256), 256), :]
        value = matmul(high, block) + matmul(low, block)
        basis_ref[pl.ds(pl.multiple_of(g * 256 + 2 * rank, 64), 256), :] = value.astype(BF16)
        return carry

    lax.fori_loop(0, groups, rotate, 0)
    acc[...] = jnp.zeros_like(acc)

    def step(g, carry):
        tile = basis_tile(basis_ref, g, rank)
        for h in range(2):

            @pl.when(needed(half_ref, count, pairs, h, g))
            def _():
                part = matmul(lt_ref[h], tile, NT)
                acc[h, pl.ds(2 * g + 1, pairs)] += part.reshape(pairs, mm, 256)

        return carry

    lax.fori_loop(0, groups + 1, step, 0)
    for e in range(count):
        h = half_ref[e]
        here = acc[h, pl.ds(pairs * e + 1, pairs), :, :128]
        before = acc[h, pl.ds(pairs * e, pairs), :, 128:]
        out_ref[e] = (here + before).astype(BF16)


def project(halves, sketches, lag_t, count):
    pieces = len(sketches)
    rows, kk, _ = sketches[0].shape
    rank = kk * pieces
    mm = 128 // pieces
    pairs = lag_t.shape[1] // mm
    return pl.pallas_call(
        functools.partial(project_kernel, count, pieces),
        out_shape=[
            jax.ShapeDtypeStruct(((rows + 5) * rank, 128), BF16),
            jax.ShapeDtypeStruct((count, pairs, mm, 128), BF16),
        ],
        in_specs=[pl.BlockSpec(memory_space=pltpu.SMEM)]
        + [pl.BlockSpec(memory_space=pltpu.VMEM)] * (pieces + 1),
        out_specs=[pl.BlockSpec(memory_space=pltpu.VMEM)] * 2,
        scratch_shapes=[
            pltpu.VMEM((rows * rank, 128), BF16),
            pltpu.VMEM((2, pairs * count + 1, mm, 256), F32),
        ],
        compiler_params=pltpu.CompilerParams(vmem_limit_bytes=VMEM_LIMIT),
        name="project",
    )(halves, *sketches, lag_t)


def totals_kernel(count, half_ref, *refs):
    p_refs = refs[:count]
    basis_ref, lt_ref, inv_ref, out_ref, wide, acc = refs[count:]
    pairs, mm, _ = p_refs[0].shape
    span = pairs * mm
    groups = inv_ref.shape[0] and (basis_ref.shape[0] // 64 - 5) // 4
    for h in range(2):
        wide[h, pl.ds(count * span - mm, mm), 128:] = jnp.zeros((mm, 128), BF16)
    for e in range(count):
        block = p_refs[e][...].reshape(span, 128)
        zero = jnp.zeros_like(block)
        for h in range(2):
            kept = jnp.where(half_ref[e] == h, block, zero)
            wide[h, pl.ds(e * span, span), :128] = kept
            if e == 0:
                wide[h, pl.ds(0, span - mm), 128:] = kept[mm:]
            else:
                wide[h, pl.ds(e * span - mm, span), 128:] = kept
    acc[...] = jnp.zeros_like(acc)

    def step(g, carry):
        tile = basis_tile(basis_ref, g, 64)
        for h in range(2):

            @pl.when(needed(half_ref, count, pairs, h, g))
            def _():
                rows = wide[h, pl.ds(pl.multiple_of(g * 2 * mm, 32), span), :]
                acc[h] += matmul(rows, tile)

        return carry

    lax.fori_loop(0, groups + 1, step, 0)
    for h in range(2):
        scaled = acc[h].reshape(pairs, mm, 256) * inv_ref[h]
        out_ref[h] = (scaled.reshape(span, 256) - SHARE * lt_ref[h].astype(F32)).astype(BF16)


def totals(halves, p_blocks, basis, lag_t, inverse):
    count = len(p_blocks)
    pairs, mm, _ = p_blocks[0].shape
    span = pairs * mm
    return pl.pallas_call(
        functools.partial(totals_kernel, count),
        out_shape=jax.ShapeDtypeStruct((2, span, 256), BF16),
        in_specs=[pl.BlockSpec(memory_space=pltpu.SMEM)]
        + [pl.BlockSpec(memory_space=pltpu.VMEM)] * (count + 3),
        out_specs=pl.BlockSpec(memory_space=pltpu.VMEM),
        scratch_shapes=[
            pltpu.VMEM((2, count * span, 256), BF16),
            pltpu.VMEM((2, span, 256), F32),
        ],
        compiler_params=pltpu.CompilerParams(vmem_limit_bytes=VMEM_LIMIT),
        name="totals",
    )(halves, *p_blocks, basis, lag_t, inverse)


def merge_kernel(offsets, depth, place_ref, scale_ref, *refs):
    count = len(offsets)
    d_refs, lag_ref, out_ref, square = refs[:count], refs[count], refs[count + 1], refs[count + 2]
    mm = 128 // count
    h, step = pl.program_id(0), pl.program_id(1)
    for b in range(depth):
        for j in range(count):
            start = pl.multiple_of(place_ref[j] * mm, mm)
            square[b, pl.ds(start, mm), :] = d_refs[j][0, pl.ds(b * mm, mm), :].astype(F32)
        for i in range(2):
            a = 2 * (step * depth + b) + i
            lag = lag_ref[0, 2 * b + i].astype(F32)
            turned = square[b, :, 128 * i : 128 * (i + 1)].T
            out_ref[0, 2 * b + i] = scale_ref[0, h, a] * lag + scale_ref[1, h, a] * turned


def merge(place, scales, parts, offsets, markov):
    count = len(parts)
    halves, blocks, _, _ = markov.shape
    mm = 128 // count
    depth = 4
    steps = blocks // 2 // depth
    return pl.pallas_call(
        functools.partial(merge_kernel, tuple(offsets), depth),
        out_shape=jax.ShapeDtypeStruct(markov.shape, F32),
        grid=(halves, steps),
        in_specs=[pl.BlockSpec(memory_space=pltpu.SMEM)] * 2
        + [pl.BlockSpec((1, depth * mm, 256), lambda h, s: (h, s, 0))] * count
        + [pl.BlockSpec((1, 2 * depth, 128, 128), lambda h, s: (h, s, 0, 0))],
        out_specs=pl.BlockSpec((1, 2 * depth, 128, 128), lambda h, s: (h, s, 0, 0)),
        scratch_shapes=[pltpu.VMEM((depth, 128, 256), F32)],
        compiler_params=pltpu.CompilerParams(vmem_limit_bytes=VMEM_LIMIT),
        name="merge",
    )(place, scales, *parts, markov)


def local(markov, omega):
    n_rows, n_cols = lax.axis_size("row"), lax.axis_size("col")
    r, c = lax.axis_index("row"), lax.axis_index("col")
    _, blocks, out_rows, columns = markov.shape
    rank = omega.shape[1]
    assert out_rows == 128 and columns == 128 and rank == 64
    kk, mm = rank // n_rows, columns // n_rows
    count = n_rows + 1
    pairs = blocks // 2
    rows = blocks * n_rows
    distance = [count - 1 - e for e in range(count)]
    halves = (c - jnp.arange(count - 1, -1, -1, dtype=jnp.int32) < 0).astype(jnp.int32)

    own = omega.reshape(pairs, 2, columns, rank).transpose(0, 3, 1, 2).reshape(pairs, rank, 256)
    own = lax.dynamic_slice_in_dim(own, r * kk, kk, 1)
    got = {0: own}
    d = 1
    while len(got) < count:
        got.update({k + d: shift_col(v, d) for k, v in list(got.items()) if k + d < count})
        d *= 2
    w_blocks = [got[d] for d in distance]

    lag_t = lax.dynamic_slice_in_dim(markov, r * mm, mm, 3)
    lag_t = lag_t.reshape(2, pairs, 2, out_rows, mm).transpose(0, 1, 4, 2, 3).reshape(2, pairs * mm, 256)

    partial = sketch_part(halves, markov, w_blocks, rows)
    partial = lax.all_to_all(partial, "col", 0, 0, tiled=True)
    chunk = partial.reshape(n_cols, rows // n_cols, kk, 128).astype(F32).sum(0).astype(BF16)
    spread = jnp.broadcast_to(chunk[None], (n_cols,) + chunk.shape)
    spread = lax.all_to_all(spread, "col", 0, 0, tiled=True).reshape(rows, kk, 128)
    sketches, _ = gather_row(spread)

    basis, parts = project(halves, sketches, lag_t, count)
    mine = parts[count - 1].astype(F32)
    for d in range(1, count):
        mine = mine + shift_col(parts[count - 1 - d], -d).astype(F32)
    mine = mine.astype(BF16)
    got = {0: mine}
    d = 1
    while len(got) < count:
        got.update({k + d: shift_col(v, d) for k, v in list(got.items()) if k + d < count})
        d *= 2
    p_blocks = [got[d] for d in distance]

    total_rows, total_cols = rows, blocks * n_cols
    lag_ids = (
        jnp.arange(2, dtype=jnp.int32)[:, None] * total_cols
        + c * blocks
        + jnp.arange(blocks, dtype=jnp.int32)[None, :]
    )
    counts = jnp.maximum(
        jnp.minimum(lag_ids, total_rows - 1) - jnp.maximum(0, lag_ids - total_cols + 1) + 1, 0
    )
    inverse = 1.0 / jnp.maximum(counts.astype(F32), 1.0)
    inverse = jnp.repeat(inverse, 128, axis=1).reshape(2, pairs, 1, 256)
    part = totals(halves, p_blocks, basis, lag_t, inverse)

    parts, offsets = gather_row(part)
    place = jnp.stack([r ^ o for o in offsets]).astype(jnp.int32)
    full = counts > 0
    scales = jnp.stack([jnp.where(full, 0.5 + 0.5 * SHARE, 1.0), jnp.where(full, 0.5, 0.0)]).astype(F32)
    return merge(place, scales, parts, offsets, markov)


def solution(mesh):
    in_specs = (P(None, "col", None, None), P("col", None))
    out_specs = P(None, "col", None, None)
    return jax.shard_map(local, mesh=mesh, in_specs=in_specs, out_specs=out_specs, check_vma=False)
```

time: 770 us -> 197 us (0.26)
  waiting for transfers between devices: 420 us -> 54.9 us
  matrix products: 242 us -> 0 us
  Pallas kernels: 0 us -> 62.3 us
  other arithmetic: 20.1 us -> 3.17 us
  between operations: 14.5 us -> 0.16 us
  starting transfers between devices: 15.3 us -> 26 us
    dot_general x122 -> x0, matrix products: 242 us -> none  [the longest x32 108 us: add_row(): jnp.dot(orthonormal_row_vector, column_rows, preferred_element_type=jnp.f...]
    ppermute x6 -> x18, waiting for transfers between devices: 256 us -> 54.9 us  [the longest x12 31 us: shift_col(): return lax.ppermute(x, 'col', [(i, (i + distance) % n) for i in range(n)])]
    psum x2 -> x0, waiting for transfers between devices: 163 us -> none  [the longest x1 81.7 us: local(): sketch = lax.psum(partial_value, 'col')]
    pallas_call x0 -> x4, Pallas kernels: none -> 62.3 us  [the longest x1 31.1 us: project(): pl.pallas_call(functools.partial(project_kernel, count, pieces), out_shap...]
    psum x2 -> x0, blocking collectives: 37.7 us -> none  [the longest x1 26.3 us: local(): projected_matrix = lax.psum(projected_matrix, 'row').astype(jnp.bfloat16)]
    all_to_all x0 -> x2, blocking collectives: none -> 36.6 us  [the longest x1 19.2 us: local(): partial = lax.all_to_all(partial, 'col', 0, 0, tiled=True)]
    select_n x6 -> x1, other arithmetic: 11.3 us -> 0.08 us  [local(): jnp.where(full, 0.5 + 0.5 * SHARE, 1.0)]
    ppermute x6 -> x18, starting transfers between devices: 15.2 us -> 26 us  [the longest x12 23 us: shift_col(): return lax.ppermute(x, 'col', [(i, (i + distance) % n) for i in range(n)])]
  transfers between devices with their start and end apart: 8 -> 18, of which waited for: 8 -> 11; matrix products, arithmetic and copies ran while one was open for 0% -> 4% of each run, Pallas kernels for 0% -> 0%
where the time goes in v1:
time: 197 us; the launch traced here: 196 us
  Pallas kernels  62.3 us (32%)
  waiting for transfers between devices  54.9 us (28%)
  blocking collectives  36.6 us (19%)
  starting transfers between devices  26 us (13%)
  local copies, waits for them, and re-layouts  12.7 us (6%)
  other arithmetic  3.17 us (2%)
    pallas_call x1, Pallas kernels, project(): pl.pallas_call(functools.partial(project_kernel, count, pieces), out_shap...  31.1 us
    ppermute x12, waiting for transfers between devices, shift_col(): return lax.ppermute(x, 'col', [(i, (i + distance) % n) for i in range(n)])  31 us
    ppermute x6, waiting for transfers between devices, swap_row(): return lax.ppermute(x, 'row', [(i, i ^ bit) for i in range(n)])  23.9 us
    ppermute x12, starting transfers between devices, shift_col(): return lax.ppermute(x, 'col', [(i, (i + distance) % n) for i in range(n)])  23 us
    all_to_all x1, blocking collectives, local(): partial = lax.all_to_all(partial, 'col', 0, 0, tiled=True)  19.2 us
    all_to_all x1, blocking collectives, local(): lax.all_to_all(spread, 'col', 0, 0, tiled=True).reshape(rows, kk, 128)  17.4 us
    pallas_call x1, Pallas kernels, totals(): pl.pallas_call(functools.partial(totals_kernel, count), out_shape=jax.Sha...  13.4 us
    pallas_call x1, Pallas kernels, sketch_part(): pl.pallas_call(functools.partial(sketch_kernel, count), out_shape=jax.Sha...  10.4 us
  transfers between devices with their start and end apart: 18, of which 11 were waited for; matrix products, arithmetic and copies ran while one was open for 4% of the time, Pallas kernels for 0%

profile of v1, /device:TPU:0, one launch (start us, length us, event | category | flops | bytes accessed | tf_op | source)
XLA Modules:
  0.0 195.9 jit_solution(13027814717761048667)
XLA Ops:
  2.3 3.0 %collective-permute-start.1 = (bf16[16,16,256]{2,1,0:T(8,128)(2,1)S(1)}, bf16[16,16,256]{2,1,0:T(8,128)(2,1)S(1)}, u32[]{:S(2)}, u32[]{:S(2)}) collective-permute-start(bf16[16,16,256]{2,1,0:T(8,128)(2,1)S(1)} %constant_dynamic-slice_fusion.1.refs_4_), channel_id=1, source_target_pairs={{0,1},{1,2},{2,3},{3,4},{4,5},{5,6},{6,7},{7,0},{8,9},{9,10},{10,1... | collective-permute-start | bytes 393224 | tf_op jit(solution)/shard_map/ppermute | solution.py:28
  5.3 1.6 collective-permute-start.3
  6.9 2.6 %collective-permute-start = (bf16[16,16,256]{2,1,0:T(8,128)(2,1)S(1)}, bf16[16,16,256]{2,1,0:T(8,128)(2,1)S(1)}, u32[]{:S(2)}, u32[]{:S(2)}) collective-permute-start(bf16[16,16,256]{2,1,0:T(8,128)(2,1)S(1)} %constant_dynamic-slice_fusion.1.refs_4_), channel_id=1, source_target_pairs={{0,4},{1,5},{2,6},{3,7},{4,0},{5,1},{6,2},{7,3},{8,12},{9,13},{10,... | collective-permute-start | bytes 393224 | tf_op jit(solution)/shard_map/ppermute | solution.py:28
  9.5 3.3 %collective-permute-done.1.refs_3_ = bf16[16,16,256]{2,1,0:T(8,128)(2,1)S(1)} collective-permute-done((bf16[16,16,256]{2,1,0:T(8,128)(2,1)S(1)}, bf16[16,16,256]{2,1,0:T(8,128)(2,1)S(1)}, u32[]{:S(2)}, u32[]{:S(2)}) %collective-permute-start.1) | collective-permute-done | bytes 131104 | tf_op jit(solution)/shard_map/ppermute | solution.py:28
  13.6 7.0 %collective-permute-done.refs_0_ = bf16[16,16,256]{2,1,0:T(8,128)(2,1)S(1)} collective-permute-done((bf16[16,16,256]{2,1,0:T(8,128)(2,1)S(1)}, bf16[16,16,256]{2,1,0:T(8,128)(2,1)S(1)}, u32[]{:S(2)}, u32[]{:S(2)}) %collective-permute-start) | collective-permute-done | bytes 131104 | tf_op jit(solution)/shard_map/ppermute | solution.py:28
  21.9 10.4 %sketch.1 = bf16[128,16,128]{2,1,0:T(8,128)(2,1)} custom-call(s32[5]{0:T(128)} %compare_convert_fusion.half_ref, bf16[2,32,128,128]{3,2,1,0:T(8,128)(2,1)} %refs_4_.1, bf16[16,16,256]{2,1,0:T(8,128)(2,1)} %copy-done.13, bf16[16,16,256]{2,1,0:T(8,128)(2,1)} %copy-done.15, bf16[16,16,256]{2,1,0:T(8,128)(2,1)} %copy-done.11, bf16[16,16,256]{2,1,0:T(8,128)(2,1)} %copy-done.9, ...), custom_call_target="tpu_custom_call" | custom-call | tf_op jit(solution)/shard_map/sketch/pallas_call | solution.py:90
  32.3 19.2 %all_to_all.10 = bf16[128,16,128]{2,1,0:T(8,128)(2,1)S(1)} all-to-all(bf16[128,16,128]{2,1,0:T(8,128)(2,1)} %sketch.1), channel_id=1, replica_groups=mesh['row'=4,'col'=8] {'col'}, dimensions={0} | all-to-all | bytes 1048576 | tf_op jit(solution)/shard_map/all_to_all | solution.py:346
  51.6 17.4 %all_to_all.11 = bf16[8,16,16,128]{3,2,1,0:T(8,128)(2,1)S(1)} all-to-all(bf16[8,16,16,128]{3,2,1,0:T(8,128)(2,1)S(1)} %broadcast_in_dim.31), channel_id=1, replica_groups=mesh['row'=4,'col'=8] {'col'}, dimensions={0} | all-to-all | bytes 1048576 | tf_op jit(solution)/shard_map/all_to_all | solution.py:349
  70.5 10.9 %collective-permute-done.4.refs_1_ = bf16[128,16,128]{2,1,0:T(8,128)(2,1)S(1)} collective-permute-done((bf16[128,16,128]{2,1,0:T(8,128)(2,1)S(1)}, bf16[128,16,128]{2,1,0:T(8,128)(2,1)S(1)}, u32[]{:S(2)}, u32[]{:S(2)}) %collective-permute-start.4) | collective-permute-done | bytes 524320 | tf_op jit(solution)/shard_map/ppermute | solution.py:33
  81.4 2.0 %constant_dynamic-slice_fusion = bf16[2,32,128,32]{3,2,1,0:T(8,128)(2,1)} fusion(bf16[2,32,128,128]{3,2,1,0:T(8,128)(2,1)S(1)} %copy-done, s32[]{:T(128)S(6)} %select_n.30), kind=kLoop, calls=%fused_computation.17 | loop fusion | bytes 1048580 | tf_op jit(solution)/shard_map/dynamic_slice | solution.py:342
  83.4 3.0 %copy.6 = bf16[2,16,32,2,128]{4,3,2,1,0:T(2,128)(2,1)S(1)} copy(bf16[2,16,32,2,128]{2,4,3,1,0:T(8,128)(2,1)} %bitcast.27) | data formatting | bytes 1048576 | tf_op jit(solution)/shard_map/transpose | solution.py:343
  87.6 31.1 %project.1 = (bf16[8512,128]{1,0:T(8,128)(2,1)}, bf16[5,16,32,128]{3,2,1,0:T(8,128)(2,1)}) custom-call(s32[5]{0:T(128)} %compare_convert_fusion.half_ref, bf16[128,16,128]{2,1,0:T(8,128)(2,1)} %bitcast.32, bf16[128,16,128]{2,1,0:T(8,128)(2,1)} %copy-done.7, bf16[128,16,128]{2,1,0:T(8,128)(2,1)} %collective-permute-done.5.refs_2_, ...), custom_call_target="tpu_custom_call" | custom-call | tf_op jit(solution)/shard_map/project/pallas_call | solution.py:210
  121.8 2.5 %collective-permute-start.9 = (bf16[16,32,128]{2,1,0:T(8,128)(2,1)S(1)}, bf16[16,32,128]{2,1,0:T(8,128)(2,1)S(1)}, u32[]{:S(2)}, u32[]{:S(2)}) collective-permute-start(bf16[16,32,128]{2,1,0:T(8,128)(2,1)S(1)} %get-tuple-element.11), channel_id=1, source_target_pairs={{0,5},{1,6},{2,7},{3,0},{4,1},{5,2},{6,3},{7,4},{8,13},{9,14},{10,... | collective-permute-start | bytes 393224 | tf_op jit(solution)/shard_map/ppermute | solution.py:28
  125.3 2.8 %collective-permute-done.7 = bf16[16,32,128]{2,1,0:T(8,128)(2,1)S(1)} collective-permute-done((bf16[16,32,128]{2,1,0:T(8,128)(2,1)S(1)}, bf16[16,32,128]{2,1,0:T(8,128)(2,1)S(1)}, u32[]{:S(2)}, u32[]{:S(2)}) %collective-permute-start.7) | collective-permute-done | bytes 131104 | tf_op jit(solution)/shard_map/ppermute | solution.py:28
  128.1 6.5 %collective-permute-done.10 = bf16[16,32,128]{2,1,0:T(8,128)(2,1)S(1)} collective-permute-done((bf16[16,32,128]{2,1,0:T(8,128)(2,1)S(1)}, bf16[16,32,128]{2,1,0:T(8,128)(2,1)S(1)}, u32[]{:S(2)}, u32[]{:S(2)}) %collective-permute-start.10) | collective-permute-done | bytes 131104 | tf_op jit(solution)/shard_map/ppermute | solution.py:28
  135.6 4.3 %collective-permute-start.12 = (bf16[16,32,128]{2,1,0:T(8,128)(2,1)S(1)}, bf16[16,32,128]{2,1,0:T(8,128)(2,1)S(1)}, u32[]{:S(2)}, u32[]{:S(2)}) collective-permute-start(bf16[16,32,128]{2,1,0:T(8,128)(2,1)S(1)} %fusion.3.refs_4_), channel_id=1, source_target_pairs={{0,1},{1,2},{2,3},{3,4},{4,5},{5,6},{6,7},{7,0},{8,9},{9,10},{10,1... | collective-permute-start | bytes 393224 | tf_op jit(solution)/shard_map/ppermute | solution.py:28
  139.9 1.5 collective-permute-start.14
  141.4 4.5 %collective-permute-start.11 = (bf16[16,32,128]{2,1,0:T(8,128)(2,1)S(1)}, bf16[16,32,128]{2,1,0:T(8,128)(2,1)S(1)}, u32[]{:S(2)}, u32[]{:S(2)}) collective-permute-start(bf16[16,32,128]{2,1,0:T(8,128)(2,1)S(1)} %fusion.3.refs_4_), channel_id=1, source_target_pairs={{0,4},{1,5},{2,6},{3,7},{4,0},{5,1},{6,2},{7,3},{8,12},{9,13},{10,... | collective-permute-start | bytes 393224 | tf_op jit(solution)/shard_map/ppermute | solution.py:28
  146.0 3.3 %collective-permute-done.12.refs_3_ = bf16[16,32,128]{2,1,0:T(8,128)(2,1)S(1)} collective-permute-done((bf16[16,32,128]{2,1,0:T(8,128)(2,1)S(1)}, bf16[16,32,128]{2,1,0:T(8,128)(2,1)S(1)}, u32[]{:S(2)}, u32[]{:S(2)}) %collective-permute-start.12) | collective-permute-done | bytes 131104 | tf_op jit(solution)/shard_map/ppermute | solution.py:28
  149.9 7.4 %collective-permute-done.11.refs_0_ = bf16[16,32,128]{2,1,0:T(8,128)(2,1)S(1)} collective-permute-done((bf16[16,32,128]{2,1,0:T(8,128)(2,1)S(1)}, bf16[16,32,128]{2,1,0:T(8,128)(2,1)S(1)}, u32[]{:S(2)}, u32[]{:S(2)}) %collective-permute-start.11) | collective-permute-done | bytes 131104 | tf_op jit(solution)/shard_map/ppermute | solution.py:28
  158.0 13.4 %totals.1.refs_0_ = bf16[2,512,256]{2,1,0:T(8,128)(2,1)} custom-call(s32[5]{0:T(128)} %compare_convert_fusion.half_ref, bf16[16,32,128]{2,1,0:T(8,128)(2,1)} %copy-done.12, bf16[16,32,128]{2,1,0:T(8,128)(2,1)} %copy-done.14, bf16[16,32,128]{2,1,0:T(8,128)(2,1)} %copy-done.10, bf16[16,32,128]{2,1,0:T(8,128)(2,1)} %copy-done.8, ...), custom_call_target="tpu_custom_call" | custom-call | tf_op jit(solution)/shard_map/totals/pallas_call | solution.py:269
  171.5 1.5 collective-permute-start.15
  173.0 12.5 %collective-permute-done.15.refs_1_ = bf16[2,512,256]{2,1,0:T(8,128)(2,1)S(1)} collective-permute-done((bf16[2,512,256]{2,1,0:T(8,128)(2,1)}, bf16[2,512,256]{2,1,0:T(8,128)(2,1)S(1)}, u32[]{:S(2)}, u32[]{:S(2)}) %collective-permute-start.15) | collective-permute-done | bytes 524320 | tf_op jit(solution)/shard_map/ppermute | solution.py:33
  188.5 7.4 %merge.1 = f32[2,32,128,128]{3,2,1,0:T(8,128)} custom-call(s32[4]{0:T(128)} %pad_add_fusion.place_ref, f32[2,2,32]{2,1,0:T(2,128)} %pad_maximum_fusion.scale_ref, bf16[2,512,256]{2,1,0:T(8,128)(2,1)} %totals.1.refs_0_, bf16[2,512,256]{2,1,0:T(8,128)(2,1)} %copy-done.2, bf16[2,512,256]{2,1,0:T(8,128)(2,1)} %copy-done.3, bf16[2,512,256]{2,1,0:T(8,128)(2,1)} %copy-done.4, ...), custom_call_target="tpu_custom_call" | custom-call | tf_op jit(solution)/shard_map/merge/pallas_call | solution.py:306
  (68 shorter events, 16.4 us)
Async XLA Ops:
  2.3 18.3 %copy-start.5 = (bf16[16,16,256]{2,1,0:T(8,128)(2,1)}, bf16[16,16,256]{2,1,0:T(8,128)(2,1)S(1)}, u32[]{:S(2)}) copy-start(bf16[16,16,256]{2,1,0:T(8,128)(2,1)S(1)} %constant_dynamic-slice_fusion.1.refs_4_) | copy-start | bytes 393220
  2.3 10.5 %collective-permute-start.1 = (bf16[16,16,256]{2,1,0:T(8,128)(2,1)S(1)}, bf16[16,16,256]{2,1,0:T(8,128)(2,1)S(1)}, u32[]{:S(2)}, u32[]{:S(2)}) collective-permute-start(bf16[16,16,256]{2,1,0:T(8,128)(2,1)S(1)} %constant_dynamic-slice_fusion.1.refs_4_), channel_id=1, source_target_pairs={{0,1},{1,2},{2,3},{3,4},{4,5},{5,6},{6,7},{7,0},{8,9},{9,10},{10,1... | collective-permute-start | bytes 393224 | tf_op jit(solution)/shard_map/ppermute | solution.py:28
  5.3 8.3 %collective-permute-start.3 = (bf16[16,16,256]{2,1,0:T(8,128)(2,1)S(1)}, bf16[16,16,256]{2,1,0:T(8,128)(2,1)S(1)}, u32[]{:S(2)}, u32[]{:S(2)}) collective-permute-start(bf16[16,16,256]{2,1,0:T(8,128)(2,1)S(1)} %constant_dynamic-slice_fusion.1.refs_4_), channel_id=1, source_target_pairs={{0,2},{1,3},{2,4},{3,5},{4,6},{5,7},{6,0},{7,1},{8,10},{9,11},{10,... | collective-permute-start | bytes 393224 | tf_op jit(solution)/shard_map/ppermute | solution.py:28
  6.9 13.7 %collective-permute-start = (bf16[16,16,256]{2,1,0:T(8,128)(2,1)S(1)}, bf16[16,16,256]{2,1,0:T(8,128)(2,1)S(1)}, u32[]{:S(2)}, u32[]{:S(2)}) collective-permute-start(bf16[16,16,256]{2,1,0:T(8,128)(2,1)S(1)} %constant_dynamic-slice_fusion.1.refs_4_), channel_id=1, source_target_pairs={{0,4},{1,5},{2,6},{3,7},{4,0},{5,1},{6,2},{7,3},{8,12},{9,13},{10,... | collective-permute-start | bytes 393224 | tf_op jit(solution)/shard_map/ppermute | solution.py:28
  12.8 7.8 %collective-permute-start.2 = (bf16[16,16,256]{2,1,0:T(8,128)(2,1)S(1)}, bf16[16,16,256]{2,1,0:T(8,128)(2,1)S(1)}, u32[]{:S(2)}, u32[]{:S(2)}) collective-permute-start(bf16[16,16,256]{2,1,0:T(8,128)(2,1)S(1)} %collective-permute-done.1.refs_3_), channel_id=1, source_target_pairs={{0,2},{1,3},{2,4},{3,5},{4,6},{5,7},{6,0},{7,1},{8,10},{9,11},{10,... | collective-permute-start | bytes 393224 | tf_op jit(solution)/shard_map/ppermute | solution.py:28
  32.3 49.2 %copy-start = (bf16[2,32,128,128]{3,2,1,0:T(8,128)(2,1)S(1)}, bf16[2,32,128,128]{3,2,1,0:T(8,128)(2,1)}, u32[]{:S(2)}) copy-start(bf16[2,32,128,128]{3,2,1,0:T(8,128)(2,1)} %refs_4_.1) | copy-start | bytes 6291460
  69.0 14.4 %copy-start.1 = (bf16[8,16,16,128]{3,2,1,0:T(8,128)(2,1)}, bf16[8,16,16,128]{3,2,1,0:T(8,128)(2,1)S(1)}, u32[]{:S(2)}) copy-start(bf16[8,16,16,128]{3,2,1,0:T(8,128)(2,1)S(1)} %all_to_all.11) | copy-start | bytes 1572868
  69.0 12.4 %collective-permute-start.4 = (bf16[128,16,128]{2,1,0:T(8,128)(2,1)S(1)}, bf16[128,16,128]{2,1,0:T(8,128)(2,1)S(1)}, u32[]{:S(2)}, u32[]{:S(2)}) collective-permute-start(bf16[128,16,128]{2,1,0:T(8,128)(2,1)S(1)} %bitcast.30), channel_id=1, source_target_pairs={{0,16},{8,24},{16,0},{24,8},{1,17},{9,25},{17,1},{25,9},{2,18},{10... | collective-permute-start | bytes 1572872 | tf_op jit(solution)/shard_map/ppermute | solution.py:33
  70.5 17.1 %collective-permute-start.5 = (bf16[128,16,128]{2,1,0:T(8,128)(2,1)S(1)}, bf16[128,16,128]{2,1,0:T(8,128)(2,1)}, u32[]{:S(2)}, u32[]{:S(2)}) collective-permute-start(bf16[128,16,128]{2,1,0:T(8,128)(2,1)S(1)} %bitcast.31), channel_id=1, source_target_pairs={{0,8},{8,0},{16,24},{24,16},{1,9},{9,1},{17,25},{25,17},{2,10},{10... | collective-permute-start | bytes 1572872 | tf_op jit(solution)/shard_map/ppermute | solution.py:33
  81.4 6.2 %collective-permute-start.6 = (bf16[128,16,128]{2,1,0:T(8,128)(2,1)S(1)}, bf16[128,16,128]{2,1,0:T(8,128)(2,1)}, u32[]{:S(2)}, u32[]{:S(2)}) collective-permute-start(bf16[128,16,128]{2,1,0:T(8,128)(2,1)S(1)} %collective-permute-done.4.refs_1_), channel_id=1, source_target_pairs={{0,8},{8,0},{16,24},{24,16},{1,9},{9,1},{17,25},{25,17},{2,10},{10... | collective-permute-start | bytes 1572872 | tf_op jit(solution)/shard_map/ppermute | solution.py:33
  119.9 8.2 %collective-permute-start.7 = (bf16[16,32,128]{2,1,0:T(8,128)(2,1)S(1)}, bf16[16,32,128]{2,1,0:T(8,128)(2,1)S(1)}, u32[]{:S(2)}, u32[]{:S(2)}) collective-permute-start(bf16[16,32,128]{2,1,0:T(8,128)(2,1)S(1)} %get-tuple-element.9), channel_id=1, source_target_pairs={{0,7},{1,0},{2,1},{3,2},{4,3},{5,4},{6,5},{7,6},{8,15},{9,8},{10,9... | collective-permute-start | bytes 393224 | tf_op jit(solution)/shard_map/ppermute | solution.py:28
  121.2 13.4 %collective-permute-start.10 = (bf16[16,32,128]{2,1,0:T(8,128)(2,1)S(1)}, bf16[16,32,128]{2,1,0:T(8,128)(2,1)S(1)}, u32[]{:S(2)}, u32[]{:S(2)}) collective-permute-start(bf16[16,32,128]{2,1,0:T(8,128)(2,1)S(1)} %get-tuple-element.10), channel_id=1, source_target_pairs={{0,4},{1,5},{2,6},{3,7},{4,0},{5,1},{6,2},{7,3},{8,12},{9,13},{10,... | collective-permute-start | bytes 393224 | tf_op jit(solution)/shard_map/ppermute | solution.py:28
  121.8 12.8 %collective-permute-start.9 = (bf16[16,32,128]{2,1,0:T(8,128)(2,1)S(1)}, bf16[16,32,128]{2,1,0:T(8,128)(2,1)S(1)}, u32[]{:S(2)}, u32[]{:S(2)}) collective-permute-start(bf16[16,32,128]{2,1,0:T(8,128)(2,1)S(1)} %get-tuple-element.11), channel_id=1, source_target_pairs={{0,5},{1,6},{2,7},{3,0},{4,1},{5,2},{6,3},{7,4},{8,13},{9,14},{10,... | collective-permute-start | bytes 393224 | tf_op jit(solution)/shard_map/ppermute | solution.py:28
  124.3 10.3 %collective-permute-start.8 = (bf16[16,32,128]{2,1,0:T(8,128)(2,1)S(1)}, bf16[16,32,128]{2,1,0:T(8,128)(2,1)S(1)}, u32[]{:S(2)}, u32[]{:S(2)}) collective-permute-start(bf16[16,32,128]{2,1,0:T(8,128)(2,1)S(1)} %get-tuple-element.12), channel_id=1, source_target_pairs={{0,6},{1,7},{2,0},{3,1},{4,2},{5,3},{6,4},{7,5},{8,14},{9,15},{10,... | collective-permute-start | bytes 393224 | tf_op jit(solution)/shard_map/ppermute | solution.py:28
  135.6 22.4 %copy-start.6 = (bf16[16,32,128]{2,1,0:T(8,128)(2,1)}, bf16[16,32,128]{2,1,0:T(8,128)(2,1)S(1)}, u32[]{:S(2)}) copy-start(bf16[16,32,128]{2,1,0:T(8,128)(2,1)S(1)} %fusion.3.refs_4_) | copy-start | bytes 393220
  135.6 13.7 %collective-permute-start.12 = (bf16[16,32,128]{2,1,0:T(8,128)(2,1)S(1)}, bf16[16,32,128]{2,1,0:T(8,128)(2,1)S(1)}, u32[]{:S(2)}, u32[]{:S(2)}) collective-permute-start(bf16[16,32,128]{2,1,0:T(8,128)(2,1)S(1)} %fusion.3.refs_4_), channel_id=1, source_target_pairs={{0,1},{1,2},{2,3},{3,4},{4,5},{5,6},{6,7},{7,0},{8,9},{9,10},{10,1... | collective-permute-start | bytes 393224 | tf_op jit(solution)/shard_map/ppermute | solution.py:28
  139.9 9.9 %collective-permute-start.14 = (bf16[16,32,128]{2,1,0:T(8,128)(2,1)S(1)}, bf16[16,32,128]{2,1,0:T(8,128)(2,1)S(1)}, u32[]{:S(2)}, u32[]{:S(2)}) collective-permute-start(bf16[16,32,128]{2,1,0:T(8,128)(2,1)S(1)} %fusion.3.refs_4_), channel_id=1, source_target_pairs={{0,2},{1,3},{2,4},{3,5},{4,6},{5,7},{6,0},{7,1},{8,10},{9,11},{10,... | collective-permute-start | bytes 393224 | tf_op jit(solution)/shard_map/ppermute | solution.py:28
  141.4 15.9 %collective-permute-start.11 = (bf16[16,32,128]{2,1,0:T(8,128)(2,1)S(1)}, bf16[16,32,128]{2,1,0:T(8,128)(2,1)S(1)}, u32[]{:S(2)}, u32[]{:S(2)}) collective-permute-start(bf16[16,32,128]{2,1,0:T(8,128)(2,1)S(1)} %fusion.3.refs_4_), channel_id=1, source_target_pairs={{0,4},{1,5},{2,6},{3,7},{4,0},{5,1},{6,2},{7,3},{8,12},{9,13},{10,... | collective-permute-start | bytes 393224 | tf_op jit(solution)/shard_map/ppermute | solution.py:28
  149.3 8.7 %copy-start.8 = (bf16[16,32,128]{2,1,0:T(8,128)(2,1)}, bf16[16,32,128]{2,1,0:T(8,128)(2,1)S(1)}, u32[]{:S(2)}) copy-start(bf16[16,32,128]{2,1,0:T(8,128)(2,1)S(1)} %collective-permute-done.12.refs_3_) | copy-start | bytes 393220
  149.3 8.0 %collective-permute-start.13 = (bf16[16,32,128]{2,1,0:T(8,128)(2,1)S(1)}, bf16[16,32,128]{2,1,0:T(8,128)(2,1)S(1)}, u32[]{:S(2)}, u32[]{:S(2)}) collective-permute-start(bf16[16,32,128]{2,1,0:T(8,128)(2,1)S(1)} %collective-permute-done.12.refs_3_), channel_id=1, source_target_pairs={{0,2},{1,3},{2,4},{3,5},{4,6},{5,7},{6,0},{7,1},{8,10},{9,11},{10,... | collective-permute-start | bytes 393224 | tf_op jit(solution)/shard_map/ppermute | solution.py:28
  149.9 8.2 %copy-start.10 = (bf16[16,32,128]{2,1,0:T(8,128)(2,1)}, bf16[16,32,128]{2,1,0:T(8,128)(2,1)S(1)}, u32[]{:S(2)}) copy-start(bf16[16,32,128]{2,1,0:T(8,128)(2,1)S(1)} %collective-permute-done.14.refs_2_) | copy-start | bytes 393220
  171.5 14.0 %collective-permute-start.15 = (bf16[2,512,256]{2,1,0:T(8,128)(2,1)}, bf16[2,512,256]{2,1,0:T(8,128)(2,1)S(1)}, u32[]{:S(2)}, u32[]{:S(2)}) collective-permute-start(bf16[2,512,256]{2,1,0:T(8,128)(2,1)} %totals.1.refs_0_), channel_id=1, source_target_pairs={{0,16},{8,24},{16,0},{24,8},{1,17},{9,25},{17,1},{25,9},{2,18},{10... | collective-permute-start | bytes 1572872 | tf_op jit(solution)/shard_map/ppermute | solution.py:33
  173.0 14.0 %collective-permute-start.16 = (bf16[2,512,256]{2,1,0:T(8,128)(2,1)}, bf16[2,512,256]{2,1,0:T(8,128)(2,1)S(1)}, u32[]{:S(2)}, u32[]{:S(2)}) collective-permute-start(bf16[2,512,256]{2,1,0:T(8,128)(2,1)} %totals.1.refs_0_), channel_id=1, source_target_pairs={{0,8},{8,0},{16,24},{24,16},{1,9},{9,1},{17,25},{25,17},{2,10},{10... | collective-permute-start | bytes 1572872 | tf_op jit(solution)/shard_map/ppermute | solution.py:33
  185.5 1.9 collective-permute-start.17
  (10 other events, 23.1 us)

commit v2 on v1

v2 whole, which is shorter than its diff:
```python
import functools

import jax
import jax.numpy as jnp
from jax import lax
from jax.experimental import pallas as pl
from jax.experimental.pallas import tpu as pltpu
from jax.sharding import PartitionSpec as P

NS_STEPS = 8
norm_floor = 1e-06
SHARE = 0.375
F32 = jnp.float32
BF16 = jnp.bfloat16
HIGHEST = lax.Precision.HIGHEST
VMEM_LIMIT = 56 * 1024 * 1024

NT = (((1,), (1,)), ((), ()))
NN = (((1,), (0,)), ((), ()))


def matmul(left, right, dims=NN):
    return lax.dot_general(left, right, dims, preferred_element_type=F32)


def shift_col(x, distance):
    n = lax.axis_size("col")
    return lax.ppermute(x, "col", [(i, (i + distance) % n) for i in range(n)])


def swap_row(x, bit):
    n = lax.axis_size("row")
    return lax.ppermute(x, "row", [(i, i ^ bit) for i in range(n)])


def gather_row(x):
    pieces, offsets = [x], [0]
    bit = lax.axis_size("row") // 2
    while bit:
        pieces = pieces + [swap_row(p, bit) for p in pieces]
        offsets = offsets + [o ^ bit for o in offsets]
        bit //= 2
    return pieces, offsets


def half_of(ids_ref, count, e):
    return jnp.where(ids_ref[1] < count - 1 - e, 1, 0)


def lag_count(lag, total_rows, total_cols):
    low = jnp.maximum(0, lag - total_cols + 1)
    return jnp.maximum(jnp.minimum(lag, total_rows - 1) - low + 1, 0)


def sketch_kernel(count, ids_ref, lag_ref, *refs):
    w_refs = refs[:count]
    out_ref, lags, padded, sems = refs[count:]
    blocks = lag_ref.shape[1]
    pairs, kk, _ = w_refs[0].shape
    copies = [
        pltpu.make_async_copy(lag_ref.at[h], lags.at[h, pl.ds(1, blocks)], sems.at[h]) for h in range(2)
    ]
    for copy in copies:
        copy.start()
    zero = jnp.zeros(lags.shape[2:], BF16)
    for h in range(2):
        lags[h, 0] = zero
        lags[h, blocks + 1] = zero
        lags[h, blocks + 2] = zero
    for e in range(count):
        padded[e, pl.ds(0, pairs)] = jnp.zeros((pairs, kk, 256), BF16)
        padded[e, pl.ds(pairs, pairs)] = w_refs[e][...]
        padded[e, pl.ds(2 * pairs, pairs + 1)] = jnp.zeros((pairs + 1, kk, 256), BF16)
    for copy in copies:
        copy.wait()

    size = pairs + 1

    def tile_of(h, t):
        before, here, after = lags[h, 2 * t], lags[h, 2 * t + 1], lags[h, 2 * t + 2]
        return jnp.concatenate(
            [jnp.concatenate([before, here], 1), jnp.concatenate([here, after], 1)], 0
        )

    def store(f, total):
        total = total.reshape(size, kk, 256).astype(BF16)
        for x in range(pairs):
            out_ref[f * 2 * pairs + 2 * x] = total[x, :, :128]
            out_ref[f * 2 * pairs + 2 * x + 1] = total[x + 1, :, 128:]

    def step(f, carry):
        low, high = half_of(ids_ref, count, f), half_of(ids_ref, count, f + 1)

        @pl.when(low == high)
        def _():
            total = jnp.zeros((size * kk, 256), F32)
            for t in range(size):
                rows = [padded[f, pl.ds(pairs + t, pairs - t)]] if t < pairs else []
                rows.append(padded[f + 1, pl.ds(pairs, t + 1)])
                rows = jnp.concatenate(rows, 0) if len(rows) > 1 else rows[0]
                total += matmul(rows.reshape(size * kk, 256), tile_of(low, t), NT)
            store(f, total)

        @pl.when(low != high)
        def _():
            total = jnp.zeros((size * kk, 256), F32)
            for side, h in enumerate((low, high)):
                for t in range(size):
                    first = t if side else pairs + t
                    rows = padded[f + side, pl.ds(first, size)].reshape(size * kk, 256)
                    total += matmul(rows, tile_of(h, t), NT)
            store(f, total)

        return carry

    lax.fori_loop(0, count - 1, step, 0)


def sketch_part(ids, markov, w_blocks, rows):
    count = len(w_blocks)
    blocks = markov.shape[1]
    pairs, kk, _ = w_blocks[0].shape
    return pl.pallas_call(
        functools.partial(sketch_kernel, count),
        out_shape=jax.ShapeDtypeStruct((rows, kk, 128), BF16),
        in_specs=[pl.BlockSpec(memory_space=pltpu.SMEM), pl.BlockSpec(memory_space=pl.ANY)]
        + [pl.BlockSpec(memory_space=pltpu.VMEM)] * count,
        out_specs=pl.BlockSpec(memory_space=pltpu.VMEM),
        scratch_shapes=[
            pltpu.VMEM((2, blocks + 3, 128, 128), BF16),
            pltpu.VMEM((count, 3 * pairs + 1, kk, 256), BF16),
            pltpu.SemaphoreType.DMA((2,)),
        ],
        compiler_params=pltpu.CompilerParams(vmem_limit_bytes=VMEM_LIMIT),
        name="sketch",
    )(ids, markov, *w_blocks)


def split(x):
    high = x.astype(BF16)
    return high, (x - high.astype(F32)).astype(BF16)


def full_dot(left, right):
    return jnp.dot(left, right, precision=HIGHEST, preferred_element_type=F32)


def newton_schulz(gram):
    size = gram.shape[0]
    row = lax.broadcasted_iota(jnp.int32, (size, size), 0)
    col = lax.broadcasted_iota(jnp.int32, (size, size), 1)
    eye = jnp.where(row == col, 1.0, 0.0)
    scale = 1.0 / jnp.sqrt(jnp.sum(gram * eye, keepdims=True) + norm_floor)
    inner = gram * (scale * scale)
    coeffs = eye * scale
    for sweep in range(NS_STEPS):
        update = 1.5 * eye - 0.5 * inner
        coeffs = full_dot(coeffs, update)
        if sweep + 1 < NS_STEPS:
            inner = full_dot(full_dot(inner, update), update)
    return coeffs


def basis_tile(basis_ref, g, rank):
    low = g * 256 if isinstance(g, int) else pl.multiple_of(g * 256, 256)
    return jnp.concatenate(
        [basis_ref[pl.ds(low + rank, 256), :], basis_ref[pl.ds(low, 256), :]], 1
    )


def project_kernel(count, pieces, ids_ref, *refs):
    s_refs = refs[:pieces]
    lt_ref, basis_ref = refs[pieces : pieces + 2]
    out_refs = refs[pieces + 2 : pieces + 2 + count]
    sketch, gram4, padded = refs[pieces + 2 + count :]
    rows, kk, _ = s_refs[0].shape
    rank = kk * pieces
    group = 256 // rank
    pairs, mm, _ = out_refs[0].shape
    groups = rows // group
    batch = 8

    gram4[...] = jnp.zeros_like(gram4)
    for h in range(2):
        padded[h, pl.ds(0, pairs - 1)] = jnp.zeros((pairs - 1, mm, 256), BF16)
        padded[h, pl.ds(pairs - 1, pairs)] = lt_ref[h].reshape(pairs, mm, 256)
        padded[h, pl.ds(2 * pairs - 1, pairs)] = jnp.zeros((pairs, mm, 256), BF16)

    def load(s, carry):
        blocks = []
        for k in range(batch):
            g = s * batch + k
            block = jnp.concatenate(
                [s_refs[j][group * g + i] for i in range(group) for j in range(pieces)], 0
            )
            sketch[pl.ds(pl.multiple_of(g * 256, 256), 256), :] = block
            blocks.append(block)
        wide = jnp.concatenate(blocks, 1)
        gram4[...] += matmul(wide, wide, NT)
        return carry

    lax.fori_loop(0, groups // batch, load, 0)
    gram = sum(
        gram4[rank * i : rank * (i + 1), rank * i : rank * (i + 1)] for i in range(group)
    )
    coeffs = newton_schulz(gram)
    wide = jnp.concatenate([coeffs] * group, 1)
    wide = jnp.concatenate([wide] * group, 0)
    row = lax.broadcasted_iota(jnp.int32, (256, 256), 0) // rank
    col = lax.broadcasted_iota(jnp.int32, (256, 256), 1) // rank
    wide = jnp.where(row == col, wide, 0.0)
    both = jnp.concatenate(split(wide), 1)

    basis_ref[pl.ds(0, 2 * rank), :] = jnp.zeros((2 * rank, 128), BF16)
    basis_ref[pl.ds((rows + 2) * rank, 3 * rank), :] = jnp.zeros((3 * rank, 128), BF16)

    def rotate(s, carry):
        for k in range(batch // 2):
            first = pl.multiple_of((s * batch + 2 * k) * 256, 256)
            block = jnp.concatenate(
                [sketch[pl.ds(first, 256), :], sketch[pl.ds(first + 256, 256), :]], 1
            )
            value = matmul(both, jnp.concatenate([block, block], 0)).astype(BF16)
            basis_ref[pl.ds(first + 2 * rank, 256), :] = value[:, :128]
            basis_ref[pl.ds(first + 2 * rank + 256, 256), :] = value[:, 128:]
        return carry

    lax.fori_loop(0, groups // batch, rotate, 0)
    half = pairs // 2

    for e in range(count):
        h = half_of(ids_ref, count, e)
        total = jnp.zeros(((pairs + 1) * mm, 256), F32)
        for k in range(pairs):
            g = half * (e - 1) + k
            if 0 <= g <= groups:
                rows_k = padded[h, pl.ds(2 * pairs - 2 - 2 * k, pairs + 1)].reshape((pairs + 1) * mm, 256)
                total += matmul(rows_k, basis_tile(basis_ref, g, rank), NT)
        total = total.reshape(pairs + 1, mm, 256)
        out_refs[e][...] = (total[1:, :, :128] + total[:-1, :, 128:]).astype(BF16)


def project(ids, sketches, lag_t, count):
    pieces = len(sketches)
    rows, kk, _ = sketches[0].shape
    rank = kk * pieces
    mm = 128 // pieces
    pairs = lag_t.shape[1] // mm
    return pl.pallas_call(
        functools.partial(project_kernel, count, pieces),
        out_shape=[
            jax.ShapeDtypeStruct(((rows + 5) * rank, 128), BF16),
        ]
        + [jax.ShapeDtypeStruct((pairs, mm, 128), BF16)] * count,
        in_specs=[pl.BlockSpec(memory_space=pltpu.SMEM)]
        + [pl.BlockSpec(memory_space=pltpu.VMEM)] * (pieces + 1),
        out_specs=[pl.BlockSpec(memory_space=pltpu.VMEM)] * (count + 1),
        scratch_shapes=[
            pltpu.VMEM((rows * rank, 128), BF16),
            pltpu.VMEM((256, 256), F32),
            pltpu.VMEM((2, 3 * pairs - 1, mm, 256), BF16),
        ],
        compiler_params=pltpu.CompilerParams(vmem_limit_bytes=VMEM_LIMIT),
        name="project",
    )(ids, *sketches, lag_t)


def totals_kernel(count, total_cols, ids_ref, *refs):
    p_refs = refs[:count]
    basis_ref, lt_ref, out_ref, wide, acc = refs[count:]
    pairs, mm, _ = p_refs[0].shape
    span = pairs * mm
    half = pairs // 2
    for h in range(2):
        wide[h, pl.ds(count * span - mm, mm), 128:] = jnp.zeros((mm, 128), BF16)
    for e in range(count):
        block = p_refs[e][...].reshape(span, 128)
        zero = jnp.zeros_like(block)
        for h in range(2):
            kept = jnp.where(half_of(ids_ref, count, e) == h, block, zero)
            wide[h, pl.ds(e * span, span), :128] = kept
            if e == 0:
                wide[h, pl.ds(0, span - mm), 128:] = kept[mm:]
            else:
                wide[h, pl.ds(e * span - mm, span), 128:] = kept
    acc[...] = jnp.zeros_like(acc)

    def chain(h, first, size):
        total = jnp.zeros((span, 256), F32)
        for k in range(size):
            start = pl.multiple_of((first + k) * 2 * mm, 32)
            total += matmul(wide[h, pl.ds(start, span), :], basis_tile(basis_ref, first + k, 64))
        acc[h] += total

    def step(e, carry):
        for h in range(2):
            here, after = half_of(ids_ref, count, e) == h, half_of(ids_ref, count, e + 1) == h

            @pl.when(jnp.logical_or(here, after))
            def _():
                chain(h, e * half, half)

        return carry

    lax.fori_loop(0, count - 1, step, 0)
    chain(0, (count - 1) * half, 1)
    blocks = 2 * pairs
    b = lax.broadcasted_iota(jnp.int32, (pairs, 1, 256), 0)
    lane = lax.broadcasted_iota(jnp.int32, (pairs, 1, 256), 2)
    for h in range(2):
        lag = h * total_cols + ids_ref[1] * blocks + 2 * b + lane // 128
        counts = lag_count(lag, blocks * (count - 1), total_cols)
        scaled = acc[h].reshape(pairs, mm, 256) * (1.0 / jnp.maximum(counts.astype(F32), 1.0))
        out_ref[h] = (scaled.reshape(span, 256) - SHARE * lt_ref[h].astype(F32)).astype(BF16)


def totals(ids, p_blocks, basis, lag_t, total_cols):
    count = len(p_blocks)
    pairs, mm, _ = p_blocks[0].shape
    span = pairs * mm
    return pl.pallas_call(
        functools.partial(totals_kernel, count, total_cols),
        out_shape=jax.ShapeDtypeStruct((2, span, 256), BF16),
        in_specs=[pl.BlockSpec(memory_space=pltpu.SMEM)]
        + [pl.BlockSpec(memory_space=pltpu.VMEM)] * (count + 2),
        out_specs=pl.BlockSpec(memory_space=pltpu.VMEM),
        scratch_shapes=[
            pltpu.VMEM((2, count * span, 256), BF16),
            pltpu.VMEM((2, span, 256), F32),
        ],
        compiler_params=pltpu.CompilerParams(vmem_limit_bytes=VMEM_LIMIT),
        name="totals",
    )(ids, *p_blocks, basis, lag_t)


def merge_kernel(offsets, depth, total_rows, total_cols, ids_ref, *refs):
    count = len(offsets)
    d_refs, lag_ref, out_ref, square = refs[:count], refs[count], refs[count + 1], refs[count + 2]
    mm = 128 // count
    h, step = pl.program_id(0), pl.program_id(1)
    blocks = 2 * depth * pl.num_programs(1)
    row = lax.broadcasted_iota(jnp.int32, (128, 128), 0)
    col = lax.broadcasted_iota(jnp.int32, (128, 128), 1)
    eye = jnp.where(row == col, 1.0, 0.0).astype(BF16)
    for j in range(count):
        start = pl.multiple_of((ids_ref[0] ^ offsets[j]) * mm, mm)
        for b in range(depth):
            square[b, pl.ds(start, mm), :] = d_refs[j][0, pl.ds(b * mm, mm), :]
    for b in range(depth):
        for i in range(2):
            a = 2 * (step * depth + b) + i
            full = lag_count(h * total_cols + ids_ref[1] * blocks + a, total_rows, total_cols) > 0
            keep = jnp.where(full, 0.5 + 0.5 * SHARE, 1.0)
            gain = jnp.where(full, 0.5, 0.0)
            turned = matmul(eye, square[b, :, 128 * i : 128 * (i + 1)], NT)
            out_ref[0, 2 * b + i] = keep * lag_ref[0, 2 * b + i].astype(F32) + gain * turned


def merge(ids, parts, offsets, markov, total_rows, total_cols):
    count = len(parts)
    halves, blocks, _, _ = markov.shape
    mm = 128 // count
    depth = blocks // 2
    steps = blocks // 2 // depth
    return pl.pallas_call(
        functools.partial(merge_kernel, tuple(offsets), depth, total_rows, total_cols),
        out_shape=jax.ShapeDtypeStruct(markov.shape, F32),
        grid=(halves, steps),
        in_specs=[pl.BlockSpec(memory_space=pltpu.SMEM)]
        + [pl.BlockSpec((1, depth * mm, 256), lambda h, s: (h, s, 0))] * count
        + [pl.BlockSpec((1, 2 * depth, 128, 128), lambda h, s: (h, s, 0, 0))],
        out_specs=pl.BlockSpec((1, 2 * depth, 128, 128), lambda h, s: (h, s, 0, 0)),
        scratch_shapes=[pltpu.VMEM((depth, 128, 256), BF16)],
        compiler_params=pltpu.CompilerParams(vmem_limit_bytes=VMEM_LIMIT),
        name="merge",
    )(ids, *parts, markov)


def spread_rounds(count):
    rounds = [[(d, [0]) for d in (1, 2) if d < count]]
    have, shift = 3, 2
    while have < count:
        last = min(have + shift, count)
        rounds.append([(shift, list(range(have - shift, last - shift)))])
        have, shift = last, shift * 2
    return rounds


def spread_blocks(own, count, extra=None):
    got = {0: own}
    for step in spread_rounds(count):
        got.update({k + d: shift_col(got[k], d) for d, ks in step for k in ks})
        if extra is not None:
            got, extra = lax.optimization_barrier((got, extra))
    return got, extra


def collect_blocks(parts, count):
    total = {d: parts[d].astype(F32) for d in range(count)}
    for step in reversed(spread_rounds(count)):
        moved = [(k, shift_col(total[k + d].astype(BF16), -d)) for d, ks in step for k in ks]
        for k, block in moved:
            total[k] = total[k] + block.astype(F32)
    return total[0].astype(BF16)


def local(markov, omega):
    n_rows, n_cols = lax.axis_size("row"), lax.axis_size("col")
    r, c = lax.axis_index("row"), lax.axis_index("col")
    _, blocks, out_rows, columns = markov.shape
    rank = omega.shape[1]
    assert out_rows == 128 and columns == 128 and rank == 64
    kk, mm = rank // n_rows, columns // n_rows
    count = n_rows + 1
    pairs = blocks // 2
    rows = blocks * n_rows
    total_cols = blocks * n_cols
    distance = [count - 1 - e for e in range(count)]
    ids = jnp.stack([r, c]).astype(jnp.int32)

    own = omega.reshape(pairs, 2, columns, rank).transpose(0, 3, 1, 2).reshape(pairs, rank, 256)
    own = lax.dynamic_slice_in_dim(own, r * kk, kk, 1)
    lag_t = lax.dynamic_slice_in_dim(markov, r * mm, mm, 3)
    lag_t = lag_t.reshape(2, pairs, 2, out_rows, mm).transpose(0, 1, 4, 2, 3).reshape(2, pairs * mm, 256)
    got, lag_t = spread_blocks(own, count, lag_t)
    w_blocks = [got[d] for d in distance]

    partial = sketch_part(ids, markov, w_blocks, rows)
    partial = lax.all_to_all(partial, "col", 0, 0, tiled=True)
    chunk = partial.reshape(n_cols, rows // n_cols, kk, 128).astype(F32).sum(0).astype(BF16)
    spread = jnp.broadcast_to(chunk[None], (n_cols,) + chunk.shape)
    spread = lax.all_to_all(spread, "col", 0, 0, tiled=True).reshape(rows, kk, 128)
    sketches, _ = gather_row(spread)

    basis, *parts = project(ids, sketches, lag_t, count)
    mine = collect_blocks({d: parts[count - 1 - d] for d in range(count)}, count)
    got, _ = spread_blocks(mine, count)
    p_blocks = [got[d] for d in distance]

    part = totals(ids, p_blocks, basis, lag_t, total_cols)
    parts, offsets = gather_row(part)
    return merge(ids, parts, offsets, markov, rows, total_cols)


def solution(mesh):
    in_specs = (P(None, "col", None, None), P("col", None))
    out_specs = P(None, "col", None, None)
    return jax.shard_map(local, mesh=mesh, in_specs=in_specs, out_specs=out_specs, check_vma=False)
```

time: 197 us -> 157 us (0.80)
  Pallas kernels: 62.3 us -> 33.2 us
  starting transfers between devices: 26 us -> 17.3 us
  blocking collectives: 36.6 us -> 34 us
    pallas_call x1, Pallas kernels: 31.1 us -> 13.8 us  [project(): pl.pallas_call(functools.partial(project_kernel, count, pieces), out_shap...]
    pallas_call x2, Pallas kernels: 20.8 us -> 12 us  [the longest x1 7.24 us: totals(): pl.pallas_call(functools.partial(totals_kernel, count, total_cols), out_s...]
    ppermute x12, starting transfers between devices: 23 us -> 14.3 us  [shift_col(): return lax.ppermute(x, 'col', [(i, (i + distance) % n) for i in range(n)])]
    pallas_call x1, Pallas kernels: 10.4 us -> 7.42 us  [sketch_part(): pl.pallas_call(functools.partial(sketch_kernel, count), out_shape=jax.Sha...]
    ppermute x12, waiting for transfers between devices: 31 us -> 33.8 us  [shift_col(): return lax.ppermute(x, 'col', [(i, (i + distance) % n) for i in range(n)])]
    all_to_all x1, blocking collectives: 19.2 us -> 16.5 us  [local(): partial = lax.all_to_all(partial, 'col', 0, 0, tiled=True)]
  transfers between devices with their start and end apart: 18 -> 18, of which waited for: 11 -> 13; matrix products, arithmetic and copies ran while one was open for 4% -> 5% of each run, Pallas kernels for 0% -> 0%
where the time goes in v2:
time: 157 us; the launch traced here: 156 us
  waiting for transfers between devices  56.5 us (36%)
  blocking collectives  34 us (22%)
  Pallas kernels  33.2 us (21%)
  starting transfers between devices  17.3 us (11%)
  local copies, waits for them, and re-layouts  11.5 us (7%)
  other arithmetic  3.5 us (2%)
    ppermute x12, waiting for transfers between devices, shift_col(): return lax.ppermute(x, 'col', [(i, (i + distance) % n) for i in range(n)])  33.8 us
    ppermute x6, waiting for transfers between devices, swap_row(): return lax.ppermute(x, 'row', [(i, i ^ bit) for i in range(n)])  22.7 us
    all_to_all x1, blocking collectives, local(): lax.all_to_all(spread, 'col', 0, 0, tiled=True).reshape(rows, kk, 128)  17.5 us
    all_to_all x1, blocking collectives, local(): partial = lax.all_to_all(partial, 'col', 0, 0, tiled=True)  16.5 us
    ppermute x12, starting transfers between devices, shift_col(): return lax.ppermute(x, 'col', [(i, (i + distance) % n) for i in range(n)])  14.3 us
    pallas_call x1, Pallas kernels, project(): pl.pallas_call(functools.partial(project_kernel, count, pieces), out_shap...  13.8 us
    pallas_call x1, Pallas kernels, sketch_part(): pl.pallas_call(functools.partial(sketch_kernel, count), out_shape=jax.Sha...  7.42 us
    pallas_call x1, Pallas kernels, totals(): pl.pallas_call(functools.partial(totals_kernel, count, total_cols), out_s...  7.24 us
  transfers between devices with their start and end apart: 18, of which 13 were waited for; matrix products, arithmetic and copies ran while one was open for 5% of the time, Pallas kernels for 0%

profile of v2, /device:TPU:0, one launch (start us, length us, event | category | flops | bytes accessed | tf_op | source)
XLA Modules:
  0.0 156.2 jit_solution(15644582482942307655)
XLA Ops:
  0.0 1.6 reshape.19
  2.4 3.1 %collective-permute-start.1 = (bf16[16,16,256]{2,1,0:T(8,128)(2,1)S(1)}, bf16[16,16,256]{2,1,0:T(8,128)(2,1)S(1)}, u32[]{:S(2)}, u32[]{:S(2)}) collective-permute-start(bf16[16,16,256]{2,1,0:T(8,128)(2,1)S(1)} %constant_dynamic-slice_fusion.1.refs_4_), channel_id=1, source_target_pairs={{0,2},{1,3},{2,4},{3,5},{4,6},{5,7},{6,0},{7,1},{8,10},{9,11},{10,... | collective-permute-start | bytes 393224 | tf_op jit(solution)/shard_map/ppermute | solution.py:28
  7.1 2.0 %constant_dynamic-slice_fusion = bf16[2,32,128,32]{3,2,1,0:T(8,128)(2,1)} fusion(bf16[2,32,128,128]{3,2,1,0:T(8,128)(2,1)S(1)} %copy-done, s32[]{:T(128)S(6)} %select_n.7), kind=kLoop, calls=%fused_computation.5 | loop fusion | bytes 1048580 | tf_op jit(solution)/shard_map/dynamic_slice | solution.py:423
  9.0 3.0 %copy.6 = bf16[2,16,32,2,128]{4,3,2,1,0:T(2,128)(2,1)S(1)} copy(bf16[2,16,32,2,128]{2,4,3,1,0:T(8,128)(2,1)} %bitcast.13) | data formatting | bytes 1048576 | tf_op jit(solution)/shard_map/transpose | solution.py:424
  13.2 1.6 %collective-permute-done.refs_3_ = bf16[16,16,256]{2,1,0:T(8,128)(2,1)S(1)} collective-permute-done((bf16[16,16,256]{2,1,0:T(8,128)(2,1)S(1)}, bf16[16,16,256]{2,1,0:T(8,128)(2,1)S(1)}, u32[]{:S(2)}, u32[]{:S(2)}) %collective-permute-start) | collective-permute-done | bytes 131104 | tf_op jit(solution)/shard_map/ppermute | solution.py:28
  14.8 1.6 %collective-permute-start.3 = (bf16[16,16,256]{2,1,0:T(8,128)(2,1)S(1)}, bf16[16,16,256]{2,1,0:T(8,128)(2,1)S(1)}, u32[]{:S(2)}, u32[]{:S(2)}) collective-permute-start(bf16[16,16,256]{2,1,0:T(8,128)(2,1)S(1)} %collective-permute-done.1.refs_2_), channel_id=1, source_target_pairs={{0,2},{1,3},{2,4},{3,5},{4,6},{5,7},{6,0},{7,1},{8,10},{9,11},{10,... | collective-permute-start | bytes 393224 | tf_op jit(solution)/shard_map/ppermute | solution.py:28
  17.0 5.5 %collective-permute-done.2.refs_1_ = bf16[16,16,256]{2,1,0:T(8,128)(2,1)S(1)} collective-permute-done((bf16[16,16,256]{2,1,0:T(8,128)(2,1)S(1)}, bf16[16,16,256]{2,1,0:T(8,128)(2,1)S(1)}, u32[]{:S(2)}, u32[]{:S(2)}) %collective-permute-start.2) | collective-permute-done | bytes 131104 | tf_op jit(solution)/shard_map/ppermute | solution.py:28
  24.5 7.4 %sketch.1 = bf16[128,16,128]{2,1,0:T(8,128)(2,1)} custom-call(s32[2]{0:T(128)} %pad_add_fusion.ids_ref, bf16[2,32,128,128]{3,2,1,0:T(8,128)(2,1)} %refs_4_.1, bf16[16,16,256]{2,1,0:T(8,128)(2,1)} %copy-done.16, bf16[16,16,256]{2,1,0:T(8,128)(2,1)} %copy-done.14, bf16[16,16,256]{2,1,0:T(8,128)(2,1)} %copy-done.10, bf16[16,16,256]{2,1,0:T(8,128)(2,1)} %copy-done.11, ...), custom_call_target="tpu_custom_call" | custom-call | tf_op jit(solution)/shard_map/sketch/pallas_call | solution.py:123
  31.9 16.5 %all_to_all.10 = bf16[128,16,128]{2,1,0:T(8,128)(2,1)S(1)} all-to-all(bf16[128,16,128]{2,1,0:T(8,128)(2,1)} %sketch.1), channel_id=1, replica_groups=mesh['row'=4,'col'=8] {'col'}, dimensions={0} | all-to-all | bytes 1048576 | tf_op jit(solution)/shard_map/all_to_all | solution.py:429
  48.6 17.5 %all_to_all.11 = bf16[8,16,16,128]{3,2,1,0:T(8,128)(2,1)S(1)} all-to-all(bf16[8,16,16,128]{3,2,1,0:T(8,128)(2,1)S(1)} %broadcast_in_dim.2), channel_id=1, replica_groups=mesh['row'=4,'col'=8] {'col'}, dimensions={0} | all-to-all | bytes 1048576 | tf_op jit(solution)/shard_map/all_to_all | solution.py:432
  67.6 11.0 %collective-permute-done.4.refs_1_ = bf16[128,16,128]{2,1,0:T(8,128)(2,1)S(1)} collective-permute-done((bf16[128,16,128]{2,1,0:T(8,128)(2,1)S(1)}, bf16[128,16,128]{2,1,0:T(8,128)(2,1)S(1)}, u32[]{:S(2)}, u32[]{:S(2)}) %collective-permute-start.4) | collective-permute-done | bytes 524320 | tf_op jit(solution)/shard_map/ppermute | solution.py:33
  78.6 1.9 %collective-permute-done.6.refs_3_ = bf16[128,16,128]{2,1,0:T(8,128)(2,1)S(1)} collective-permute-done((bf16[128,16,128]{2,1,0:T(8,128)(2,1)S(1)}, bf16[128,16,128]{2,1,0:T(8,128)(2,1)S(1)}, u32[]{:S(2)}, u32[]{:S(2)}) %collective-permute-start.6) | collective-permute-done | bytes 524320 | tf_op jit(solution)/shard_map/ppermute | solution.py:33
  81.3 13.8 %project.1 = (bf16[8512,128]{1,0:T(8,128)(2,1)}, bf16[16,32,128]{2,1,0:T(8,128)(2,1)}, bf16[16,32,128]{2,1,0:T(8,128)(2,1)}, bf16[16,32,128]{2,1,0:T(8,128)(2,1)...) custom-call(s32[2]{0:T(128)} %pad_add_fusion.ids_ref, bf16[128,16,128]{2,1,0:T(8,128)(2,1)} %bitcast.18, ...), custom_call_target="tpu_custom_call" | custom-call | tf_op jit(solution)/shard_map/project/pallas_call | solution.py:249
  95.1 2.0 %collective-permute-start.7 = (bf16[16,32,128]{2,1,0:T(8,128)(2,1)}, bf16[16,32,128]{2,1,0:T(8,128)(2,1)S(1)}, u32[]{:S(2)}, u32[]{:S(2)}) collective-permute-start(bf16[16,32,128]{2,1,0:T(8,128)(2,1)} %get-tuple-element.33), channel_id=1, source_target_pairs={{0,6},{1,7},{2,0},{3,1},{4,2},{5,3},{6,4},{7,5},{8,14},{9,15},{10,... | collective-permute-start | bytes 393224 | tf_op jit(solution)/shard_map/ppermute | solution.py:28
  97.8 3.9 %collective-permute-done.7 = bf16[16,32,128]{2,1,0:T(8,128)(2,1)S(1)} collective-permute-done((bf16[16,32,128]{2,1,0:T(8,128)(2,1)}, bf16[16,32,128]{2,1,0:T(8,128)(2,1)S(1)}, u32[]{:S(2)}, u32[]{:S(2)}) %collective-permute-start.7) | collective-permute-done | bytes 131104 | tf_op jit(solution)/shard_map/ppermute | solution.py:28
  102.6 5.0 %collective-permute-start.8 = (bf16[16,32,128]{2,1,0:T(8,128)(2,1)S(1)}, bf16[16,32,128]{2,1,0:T(8,128)(2,1)S(1)}, u32[]{:S(2)}, u32[]{:S(2)}) collective-permute-start(bf16[16,32,128]{2,1,0:T(8,128)(2,1)S(1)} %add_convert_fusion.2), channel_id=1, source_target_pairs={{0,7},{1,0},{2,1},{3,2},{4,3},{5,4},{6,5},{7,6},{8,15},{9,8},{10,9... | collective-permute-start | bytes 393224 | tf_op jit(solution)/shard_map/ppermute | solution.py:28
  108.6 2.0 %collective-permute-done.8 = bf16[16,32,128]{2,1,0:T(8,128)(2,1)S(1)} collective-permute-done((bf16[16,32,128]{2,1,0:T(8,128)(2,1)S(1)}, bf16[16,32,128]{2,1,0:T(8,128)(2,1)S(1)}, u32[]{:S(2)}, u32[]{:S(2)}) %collective-permute-start.8) | collective-permute-done | bytes 131104 | tf_op jit(solution)/shard_map/ppermute | solution.py:28
  110.6 3.0 %collective-permute-done.10 = bf16[16,32,128]{2,1,0:T(8,128)(2,1)S(1)} collective-permute-done((bf16[16,32,128]{2,1,0:T(8,128)(2,1)S(1)}, bf16[16,32,128]{2,1,0:T(8,128)(2,1)S(1)}, u32[]{:S(2)}, u32[]{:S(2)}) %collective-permute-start.10) | collective-permute-done | bytes 131104 | tf_op jit(solution)/shard_map/ppermute | solution.py:28
  114.7 8.6 %collective-permute-done.13.refs_3_ = bf16[16,32,128]{2,1,0:T(8,128)(2,1)S(1)} collective-permute-done((bf16[16,32,128]{2,1,0:T(8,128)(2,1)S(1)}, bf16[16,32,128]{2,1,0:T(8,128)(2,1)S(1)}, u32[]{:S(2)}, u32[]{:S(2)}) %collective-permute-start.13) | collective-permute-done | bytes 131104 | tf_op jit(solution)/shard_map/ppermute | solution.py:28
  123.6 6.5 %collective-permute-done.14.refs_1_ = bf16[16,32,128]{2,1,0:T(8,128)(2,1)S(1)} collective-permute-done((bf16[16,32,128]{2,1,0:T(8,128)(2,1)S(1)}, bf16[16,32,128]{2,1,0:T(8,128)(2,1)S(1)}, u32[]{:S(2)}, u32[]{:S(2)}) %collective-permute-start.14) | collective-permute-done | bytes 131104 | tf_op jit(solution)/shard_map/ppermute | solution.py:28
  132.1 7.2 %totals.1.refs_0_ = bf16[2,512,256]{2,1,0:T(8,128)(2,1)} custom-call(s32[2]{0:T(128)} %pad_add_fusion.ids_ref, bf16[16,32,128]{2,1,0:T(8,128)(2,1)} %copy-done.17, bf16[16,32,128]{2,1,0:T(8,128)(2,1)} %copy-done.15, bf16[16,32,128]{2,1,0:T(8,128)(2,1)} %copy-done.13, bf16[16,32,128]{2,1,0:T(8,128)(2,1)} %copy-done.12, bf16[16,32,128]{2,1,0:T(8,128)(2,1)} %copy-done.6, ...), custom_call_target="tpu_custom_call" | custom-call | tf_op jit(solution)/shard_map/totals/pallas_call | solution.py:321
  140.9 7.9 %collective-permute-done.15.refs_1_ = bf16[2,512,256]{2,1,0:T(8,128)(2,1)S(1)} collective-permute-done((bf16[2,512,256]{2,1,0:T(8,128)(2,1)}, bf16[2,512,256]{2,1,0:T(8,128)(2,1)S(1)}, u32[]{:S(2)}, u32[]{:S(2)}) %collective-permute-start.15) | collective-permute-done | bytes 524320 | tf_op jit(solution)/shard_map/ppermute | solution.py:33
  148.8 1.9 %collective-permute-done.17.refs_3_ = bf16[2,512,256]{2,1,0:T(8,128)(2,1)S(1)} collective-permute-done((bf16[2,512,256]{2,1,0:T(8,128)(2,1)S(1)}, bf16[2,512,256]{2,1,0:T(8,128)(2,1)S(1)}, u32[]{:S(2)}, u32[]{:S(2)}) %collective-permute-start.17) | collective-permute-done | bytes 524320 | tf_op jit(solution)/shard_map/ppermute | solution.py:33
  151.5 4.8 %merge.1 = f32[2,32,128,128]{3,2,1,0:T(8,128)} custom-call(s32[2]{0:T(128)} %pad_add_fusion.ids_ref, bf16[2,512,256]{2,1,0:T(8,128)(2,1)} %totals.1.refs_0_, bf16[2,512,256]{2,1,0:T(8,128)(2,1)} %copy-done.2, bf16[2,512,256]{2,1,0:T(8,128)(2,1)} %copy-done.3, bf16[2,512,256]{2,1,0:T(8,128)(2,1)} %copy-done.4, bf16[2,32,128,128]{3,2,1,0:T(8,128)(2,1)} %refs_4_.1), custom_call_target="tpu_custom_call" | custom-call | tf_op jit(solution)/shard_map/merge/pallas_call | solution.py:365
  (67 shorter events, 16.9 us)
Async XLA Ops:
  2.4 10.8 %collective-permute-start.1 = (bf16[16,16,256]{2,1,0:T(8,128)(2,1)S(1)}, bf16[16,16,256]{2,1,0:T(8,128)(2,1)S(1)}, u32[]{:S(2)}, u32[]{:S(2)}) collective-permute-start(bf16[16,16,256]{2,1,0:T(8,128)(2,1)S(1)} %constant_dynamic-slice_fusion.1.refs_4_), channel_id=1, source_target_pairs={{0,2},{1,3},{2,4},{3,5},{4,6},{5,7},{6,0},{7,1},{8,10},{9,11},{10,... | collective-permute-start | bytes 393224 | tf_op jit(solution)/shard_map/ppermute | solution.py:28
  5.5 9.3 %collective-permute-start = (bf16[16,16,256]{2,1,0:T(8,128)(2,1)S(1)}, bf16[16,16,256]{2,1,0:T(8,128)(2,1)S(1)}, u32[]{:S(2)}, u32[]{:S(2)}) collective-permute-start(bf16[16,16,256]{2,1,0:T(8,128)(2,1)S(1)} %constant_dynamic-slice_fusion.1.refs_4_), channel_id=1, source_target_pairs={{0,1},{1,2},{2,3},{3,4},{4,5},{5,6},{6,7},{7,0},{8,9},{9,10},{10,1... | collective-permute-start | bytes 393224 | tf_op jit(solution)/shard_map/ppermute | solution.py:28
  13.2 10.7 %copy-start.10 = (bf16[16,16,256]{2,1,0:T(8,128)(2,1)}, bf16[16,16,256]{2,1,0:T(8,128)(2,1)S(1)}, u32[]{:S(2)}) copy-start(bf16[16,16,256]{2,1,0:T(8,128)(2,1)S(1)} %collective-permute-done.1.refs_2_) | copy-start | bytes 393220
  14.8 9.1 %copy-start.11 = (bf16[16,16,256]{2,1,0:T(8,128)(2,1)}, bf16[16,16,256]{2,1,0:T(8,128)(2,1)S(1)}, u32[]{:S(2)}) copy-start(bf16[16,16,256]{2,1,0:T(8,128)(2,1)S(1)} %collective-permute-done.refs_3_) | copy-start | bytes 393220
  14.8 7.6 %collective-permute-start.2 = (bf16[16,16,256]{2,1,0:T(8,128)(2,1)S(1)}, bf16[16,16,256]{2,1,0:T(8,128)(2,1)S(1)}, u32[]{:S(2)}, u32[]{:S(2)}) collective-permute-start(bf16[16,16,256]{2,1,0:T(8,128)(2,1)S(1)} %collective-permute-done.refs_3_), channel_id=1, source_target_pairs={{0,2},{1,3},{2,4},{3,5},{4,6},{5,7},{6,0},{7,1},{8,10},{9,11},{10,... | collective-permute-start | bytes 393224 | tf_op jit(solution)/shard_map/ppermute | solution.py:28
  14.8 9.0 %collective-permute-start.3 = (bf16[16,16,256]{2,1,0:T(8,128)(2,1)S(1)}, bf16[16,16,256]{2,1,0:T(8,128)(2,1)S(1)}, u32[]{:S(2)}, u32[]{:S(2)}) collective-permute-start(bf16[16,16,256]{2,1,0:T(8,128)(2,1)S(1)} %collective-permute-done.1.refs_2_), channel_id=1, source_target_pairs={{0,2},{1,3},{2,4},{3,5},{4,6},{5,7},{6,0},{7,1},{8,10},{9,11},{10,... | collective-permute-start | bytes 393224 | tf_op jit(solution)/shard_map/ppermute | solution.py:28
  66.1 14.4 %copy-start.1 = (bf16[8,16,16,128]{3,2,1,0:T(8,128)(2,1)}, bf16[8,16,16,128]{3,2,1,0:T(8,128)(2,1)S(1)}, u32[]{:S(2)}) copy-start(bf16[8,16,16,128]{3,2,1,0:T(8,128)(2,1)S(1)} %all_to_all.11) | copy-start | bytes 1572868
  66.1 12.5 %collective-permute-start.4 = (bf16[128,16,128]{2,1,0:T(8,128)(2,1)S(1)}, bf16[128,16,128]{2,1,0:T(8,128)(2,1)S(1)}, u32[]{:S(2)}, u32[]{:S(2)}) collective-permute-start(bf16[128,16,128]{2,1,0:T(8,128)(2,1)S(1)} %bitcast.16), channel_id=1, source_target_pairs={{0,16},{8,24},{16,0},{24,8},{1,17},{9,25},{17,1},{25,9},{2,18},{10... | collective-permute-start | bytes 1572872 | tf_op jit(solution)/shard_map/ppermute | solution.py:33
  67.6 11.0 %collective-permute-start.5 = (bf16[128,16,128]{2,1,0:T(8,128)(2,1)S(1)}, bf16[128,16,128]{2,1,0:T(8,128)(2,1)S(1)}, u32[]{:S(2)}, u32[]{:S(2)}) collective-permute-start(bf16[128,16,128]{2,1,0:T(8,128)(2,1)S(1)} %bitcast.17), channel_id=1, source_target_pairs={{0,8},{8,0},{16,24},{24,16},{1,9},{9,1},{17,25},{25,17},{2,10},{10... | collective-permute-start | bytes 1572872 | tf_op jit(solution)/shard_map/ppermute | solution.py:33
  78.6 1.9 %collective-permute-start.6 = (bf16[128,16,128]{2,1,0:T(8,128)(2,1)S(1)}, bf16[128,16,128]{2,1,0:T(8,128)(2,1)S(1)}, u32[]{:S(2)}, u32[]{:S(2)}) collective-permute-start(bf16[128,16,128]{2,1,0:T(8,128)(2,1)S(1)} %collective-permute-done.4.refs_1_), channel_id=1, source_target_pairs={{0,8},{8,0},{16,24},{24,16},{1,9},{9,1},{17,25},{25,17},{2,10},{10... | collective-permute-start | bytes 1572872 | tf_op jit(solution)/shard_map/ppermute | solution.py:33
  95.1 6.6 %collective-permute-start.7 = (bf16[16,32,128]{2,1,0:T(8,128)(2,1)}, bf16[16,32,128]{2,1,0:T(8,128)(2,1)S(1)}, u32[]{:S(2)}, u32[]{:S(2)}) collective-permute-start(bf16[16,32,128]{2,1,0:T(8,128)(2,1)} %get-tuple-element.33), channel_id=1, source_target_pairs={{0,6},{1,7},{2,0},{3,1},{4,2},{5,3},{6,4},{7,5},{8,14},{9,15},{10,... | collective-permute-start | bytes 393224 | tf_op jit(solution)/shard_map/ppermute | solution.py:28
  97.1 10.6 %collective-permute-start.9 = (bf16[16,32,128]{2,1,0:T(8,128)(2,1)}, bf16[16,32,128]{2,1,0:T(8,128)(2,1)S(1)}, u32[]{:S(2)}, u32[]{:S(2)}) collective-permute-start(bf16[16,32,128]{2,1,0:T(8,128)(2,1)} %get-tuple-element.35), channel_id=1, source_target_pairs={{0,6},{1,7},{2,0},{3,1},{4,2},{5,3},{6,4},{7,5},{8,14},{9,15},{10,... | collective-permute-start | bytes 393224 | tf_op jit(solution)/shard_map/ppermute | solution.py:28
  102.6 8.0 %collective-permute-start.8 = (bf16[16,32,128]{2,1,0:T(8,128)(2,1)S(1)}, bf16[16,32,128]{2,1,0:T(8,128)(2,1)S(1)}, u32[]{:S(2)}, u32[]{:S(2)}) collective-permute-start(bf16[16,32,128]{2,1,0:T(8,128)(2,1)S(1)} %add_convert_fusion.2), channel_id=1, source_target_pairs={{0,7},{1,0},{2,1},{3,2},{4,3},{5,4},{6,5},{7,6},{8,15},{9,8},{10,9... | collective-permute-start | bytes 393224 | tf_op jit(solution)/shard_map/ppermute | solution.py:28
  108.6 5.0 %collective-permute-start.10 = (bf16[16,32,128]{2,1,0:T(8,128)(2,1)S(1)}, bf16[16,32,128]{2,1,0:T(8,128)(2,1)S(1)}, u32[]{:S(2)}, u32[]{:S(2)}) collective-permute-start(bf16[16,32,128]{2,1,0:T(8,128)(2,1)S(1)} %add_convert_fusion.1), channel_id=1, source_target_pairs={{0,6},{1,7},{2,0},{3,1},{4,2},{5,3},{6,4},{7,5},{8,14},{9,15},{10,... | collective-permute-start | bytes 393224 | tf_op jit(solution)/shard_map/ppermute | solution.py:28
  114.6 16.9 %copy-start.6 = (bf16[16,32,128]{2,1,0:T(8,128)(2,1)}, bf16[16,32,128]{2,1,0:T(8,128)(2,1)S(1)}, u32[]{:S(2)}) copy-start(bf16[16,32,128]{2,1,0:T(8,128)(2,1)S(1)} %add_convert_fusion.refs_4_) | copy-start | bytes 393220
  114.6 8.7 %collective-permute-start.13 = (bf16[16,32,128]{2,1,0:T(8,128)(2,1)S(1)}, bf16[16,32,128]{2,1,0:T(8,128)(2,1)S(1)}, u32[]{:S(2)}, u32[]{:S(2)}) collective-permute-start(bf16[16,32,128]{2,1,0:T(8,128)(2,1)S(1)} %add_convert_fusion.refs_4_), channel_id=1, source_target_pairs={{0,1},{1,2},{2,3},{3,4},{4,5},{5,6},{6,7},{7,0},{8,9},{9,10},{10,1... | collective-permute-start | bytes 393224 | tf_op jit(solution)/shard_map/ppermute | solution.py:28
  114.6 8.7 %collective-permute-start.11 = (bf16[16,32,128]{2,1,0:T(8,128)(2,1)S(1)}, bf16[16,32,128]{2,1,0:T(8,128)(2,1)S(1)}, u32[]{:S(2)}, u32[]{:S(2)}) collective-permute-start(bf16[16,32,128]{2,1,0:T(8,128)(2,1)S(1)} %add_convert_fusion.refs_4_), channel_id=1, source_target_pairs={{0,2},{1,3},{2,4},{3,5},{4,6},{5,7},{6,0},{7,1},{8,10},{9,11},{10,... | collective-permute-start | bytes 393224 | tf_op jit(solution)/shard_map/ppermute | solution.py:28
  123.3 8.2 %copy-start.12 = (bf16[16,32,128]{2,1,0:T(8,128)(2,1)}, bf16[16,32,128]{2,1,0:T(8,128)(2,1)S(1)}, u32[]{:S(2)}) copy-start(bf16[16,32,128]{2,1,0:T(8,128)(2,1)S(1)} %collective-permute-done.13.refs_3_) | copy-start | bytes 393220
  123.3 6.8 %collective-permute-start.14 = (bf16[16,32,128]{2,1,0:T(8,128)(2,1)S(1)}, bf16[16,32,128]{2,1,0:T(8,128)(2,1)S(1)}, u32[]{:S(2)}, u32[]{:S(2)}) collective-permute-start(bf16[16,32,128]{2,1,0:T(8,128)(2,1)S(1)} %collective-permute-done.13.refs_3_), channel_id=1, source_target_pairs={{0,2},{1,3},{2,4},{3,5},{4,6},{5,7},{6,0},{7,1},{8,10},{9,11},{10,... | collective-permute-start | bytes 393224 | tf_op jit(solution)/shard_map/ppermute | solution.py:28
  123.3 8.2 %copy-start.13 = (bf16[16,32,128]{2,1,0:T(8,128)(2,1)}, bf16[16,32,128]{2,1,0:T(8,128)(2,1)S(1)}, u32[]{:S(2)}) copy-start(bf16[16,32,128]{2,1,0:T(8,128)(2,1)S(1)} %collective-permute-done.11.refs_2_) | copy-start | bytes 393220
  123.3 8.2 %collective-permute-start.12 = (bf16[16,32,128]{2,1,0:T(8,128)(2,1)S(1)}, bf16[16,32,128]{2,1,0:T(8,128)(2,1)S(1)}, u32[]{:S(2)}, u32[]{:S(2)}) collective-permute-start(bf16[16,32,128]{2,1,0:T(8,128)(2,1)S(1)} %collective-permute-done.11.refs_2_), channel_id=1, source_target_pairs={{0,2},{1,3},{2,4},{3,5},{4,6},{5,7},{6,0},{7,1},{8,10},{9,11},{10,... | collective-permute-start | bytes 393224 | tf_op jit(solution)/shard_map/ppermute | solution.py:28
  139.4 9.4 %collective-permute-start.15 = (bf16[2,512,256]{2,1,0:T(8,128)(2,1)}, bf16[2,512,256]{2,1,0:T(8,128)(2,1)S(1)}, u32[]{:S(2)}, u32[]{:S(2)}) collective-permute-start(bf16[2,512,256]{2,1,0:T(8,128)(2,1)} %totals.1.refs_0_), channel_id=1, source_target_pairs={{0,16},{8,24},{16,0},{24,8},{1,17},{9,25},{17,1},{25,9},{2,18},{10... | collective-permute-start | bytes 1572872 | tf_op jit(solution)/shard_map/ppermute | solution.py:33
  140.9 7.9 %collective-permute-start.16 = (bf16[2,512,256]{2,1,0:T(8,128)(2,1)}, bf16[2,512,256]{2,1,0:T(8,128)(2,1)S(1)}, u32[]{:S(2)}, u32[]{:S(2)}) collective-permute-start(bf16[2,512,256]{2,1,0:T(8,128)(2,1)} %totals.1.refs_0_), channel_id=1, source_target_pairs={{0,8},{8,0},{16,24},{24,16},{1,9},{9,1},{17,25},{25,17},{2,10},{10... | collective-permute-start | bytes 1572872 | tf_op jit(solution)/shard_map/ppermute | solution.py:33
  148.8 1.9 %collective-permute-start.17 = (bf16[2,512,256]{2,1,0:T(8,128)(2,1)S(1)}, bf16[2,512,256]{2,1,0:T(8,128)(2,1)S(1)}, u32[]{:S(2)}, u32[]{:S(2)}) collective-permute-start(bf16[2,512,256]{2,1,0:T(8,128)(2,1)S(1)} %collective-permute-done.15.refs_1_), channel_id=1, source_target_pairs={{0,8},{8,0},{16,24},{24,16},{1,9},{9,1},{17,25},{25,17},{2,10},{10... | collective-permute-start | bytes 1572872 | tf_op jit(solution)/shard_map/ppermute | solution.py:33
  (12 other events, 27.0 us)

commit v3 on v2

v3 whole, which is shorter than its diff:
```python
import functools

import jax
import jax.numpy as jnp
from jax import lax
from jax.experimental import pallas as pl
from jax.experimental.pallas import tpu as pltpu
from jax.sharding import PartitionSpec as P


NS_STEPS = 8
norm_floor = 1e-06
SHARE = 0.375
F32 = jnp.float32
BF16 = jnp.bfloat16
HIGHEST = lax.Precision.HIGHEST
VMEM_LIMIT = 56 * 1024 * 1024

NT = (((1,), (1,)), ((), ()))
NN = (((1,), (0,)), ((), ()))


def matmul(left, right, dims=NN):
    return lax.dot_general(left, right, dims, preferred_element_type=F32)


def shift_col(x, distance):
    n = lax.axis_size("col")
    return lax.ppermute(x, "col", [(i, (i + distance) % n) for i in range(n)])


def swap(axis, x, bit):
    n = lax.axis_size(axis)
    return lax.ppermute(x, axis, [(i, i ^ bit) for i in range(n)])


def gather_row(x):
    pieces, offsets = [x], [0]
    bit = lax.axis_size("row") // 2
    while bit:
        pieces = pieces + [swap("row", p, bit) for p in pieces]
        offsets = offsets + [o ^ bit for o in offsets]
        bit //= 2
    return pieces, offsets


def half_of(ids_ref, count, e):
    return jnp.where(ids_ref[1] < count - 1 - e, 1, 0)


def lag_count(lag, total_rows, total_cols):
    low = jnp.maximum(0, lag - total_cols + 1)
    return jnp.maximum(jnp.minimum(lag, total_rows - 1) - low + 1, 0)


def sketch_kernel(count, first, last, ids_ref, lag_ref, *refs):
    w_refs = refs[: last - first + 1]
    out_ref, lags, padded, sems = refs[-4:]
    blocks = lag_ref.shape[1]
    pairs, kk, _ = w_refs[0].shape
    copies = [
        pltpu.make_async_copy(lag_ref.at[h], lags.at[h, pl.ds(1, blocks)], sems.at[h]) for h in range(2)
    ]
    for copy in copies:
        copy.start()
    zero = jnp.zeros(lags.shape[2:], BF16)
    for h in range(2):
        lags[h, 0] = zero
        lags[h, blocks + 1] = zero
        lags[h, blocks + 2] = zero
    for e in range(last - first + 1):
        padded[e, pl.ds(0, pairs)] = jnp.zeros((pairs, kk, 256), BF16)
        padded[e, pl.ds(pairs, pairs)] = w_refs[e][...]
        padded[e, pl.ds(2 * pairs, pairs + 1)] = jnp.zeros((pairs + 1, kk, 256), BF16)
    for copy in copies:
        copy.wait()

    size = pairs + 1

    def tile_of(h, t):
        before, here, after = lags[h, 2 * t], lags[h, 2 * t + 1], lags[h, 2 * t + 2]
        return jnp.concatenate(
            [jnp.concatenate([before, here], 1), jnp.concatenate([here, after], 1)], 0
        )

    def store(f, total):
        total = total.reshape(size, kk, 256).astype(BF16)
        for x in range(pairs):
            out_ref[f * 2 * pairs + 2 * x] = total[x, :, :128]
            out_ref[f * 2 * pairs + 2 * x + 1] = total[x + 1, :, 128:]

    def step(f, carry):
        low, high = half_of(ids_ref, count, first + f), half_of(ids_ref, count, first + f + 1)

        @pl.when(low == high)
        def _():
            total = jnp.zeros((size * kk, 256), F32)
            for t in range(size):
                rows = [padded[f, pl.ds(pairs + t, pairs - t)]] if t < pairs else []
                rows.append(padded[f + 1, pl.ds(pairs, t + 1)])
                rows = jnp.concatenate(rows, 0) if len(rows) > 1 else rows[0]
                total += matmul(rows.reshape(size * kk, 256), tile_of(low, t), NT)
            store(f, total)

        @pl.when(low != high)
        def _():
            total = jnp.zeros((size * kk, 256), F32)
            for side, h in enumerate((low, high)):
                for t in range(size):
                    offset = t if side else pairs + t
                    rows = padded[f + side, pl.ds(offset, size)].reshape(size * kk, 256)
                    total += matmul(rows, tile_of(h, t), NT)
            store(f, total)

        return carry

    lax.fori_loop(0, last - first, step, 0)


def sketch_part(ids, markov, w_blocks, first, last, rows, before=None):
    count = rows // markov.shape[1] + 1
    blocks = markov.shape[1]
    pairs, kk, _ = w_blocks[first].shape
    used = [w_blocks[e] for e in range(first, last + 1)]
    height = (last - first) * blocks
    place = first // (last - first)
    return pl.pallas_call(
        functools.partial(sketch_kernel, count, first, last),
        out_shape=jax.ShapeDtypeStruct((rows, kk, 128), BF16),
        grid=(1,),
        in_specs=[pl.BlockSpec(memory_space=pltpu.SMEM), pl.BlockSpec(memory_space=pl.ANY)]
        + [pl.BlockSpec(memory_space=pltpu.VMEM)] * len(used)
        + ([] if before is None else [pl.BlockSpec(memory_space=pl.ANY)]),
        out_specs=pl.BlockSpec((height, kk, 128), lambda i: (place, 0, 0)),
        input_output_aliases={} if before is None else {2 + len(used): 0},
        scratch_shapes=[
            pltpu.VMEM((2, blocks + 3, 128, 128), BF16),
            pltpu.VMEM((len(used), 3 * pairs + 1, kk, 256), BF16),
            pltpu.SemaphoreType.DMA((2,)),
        ],
        compiler_params=pltpu.CompilerParams(vmem_limit_bytes=VMEM_LIMIT),
        name="sketch",
    )(ids, markov, *used, *([] if before is None else [before]))


def split(x):
    high = x.astype(BF16)
    return high, (x - high.astype(F32)).astype(BF16)


def full_dot(left, right):
    return jnp.dot(left, right, precision=HIGHEST, preferred_element_type=F32)


def newton_schulz(gram):
    size = gram.shape[0]
    row = lax.broadcasted_iota(jnp.int32, (size, size), 0)
    col = lax.broadcasted_iota(jnp.int32, (size, size), 1)
    eye = jnp.where(row == col, 1.0, 0.0)
    scale = 1.0 / jnp.sqrt(jnp.sum(gram * eye, keepdims=True) + norm_floor)
    inner = gram * (scale * scale)
    coeffs = eye * scale
    for sweep in range(NS_STEPS):
        update = 1.5 * eye - 0.5 * inner
        coeffs = full_dot(coeffs, update)
        if sweep + 1 < NS_STEPS:
            inner = full_dot(full_dot(inner, update), update)
    return coeffs


def basis_tile(basis_ref, g, rank):
    low = g * 256 if isinstance(g, int) else pl.multiple_of(g * 256, 256)
    return jnp.concatenate(
        [basis_ref[pl.ds(low + rank, 256), :], basis_ref[pl.ds(low, 256), :]], 1
    )


def pad_lags(lt_ref, padded):
    pairs = (padded.shape[1] + 1) // 3
    mm = padded.shape[2]
    for h in range(2):
        padded[h, pl.ds(0, pairs - 1)] = jnp.zeros((pairs - 1, mm, 256), BF16)
        padded[h, pl.ds(pairs - 1, pairs)] = lt_ref[h].reshape(pairs, mm, 256)
        padded[h, pl.ds(2 * pairs - 1, pairs)] = jnp.zeros((pairs, mm, 256), BF16)


def project_block(count, rank, e, ids_ref, basis_ref, padded):
    pairs = (padded.shape[1] + 1) // 3
    mm = padded.shape[2]
    groups = (basis_ref.shape[0] // rank - 5) // (256 // rank)
    h = half_of(ids_ref, count, e)
    total = jnp.zeros(((pairs + 1) * mm, 256), F32)
    for k in range(pairs):
        g = pairs // 2 * (e - 1) + k
        if 0 <= g <= groups:
            rows_k = padded[h, pl.ds(2 * pairs - 2 - 2 * k, pairs + 1)].reshape((pairs + 1) * mm, 256)
            total += matmul(rows_k, basis_tile(basis_ref, g, rank), NT)
    total = total.reshape(pairs + 1, mm, 256)
    return (total[1:, :, :128] + total[:-1, :, 128:]).astype(BF16)


def project_rest_kernel(count, rank, ids_ref, basis_ref, lt_ref, middle_ref, own_ref, padded):
    pad_lags(lt_ref, padded)
    late = middle_ref.shape[0]
    for e in range(late, count - 1):
        middle_ref[e - late] = project_block(count, rank, e, ids_ref, basis_ref, padded)
    own_ref[...] = project_block(count, rank, count - 1, ids_ref, basis_ref, padded)


def project_kernel(count, pieces, ids_ref, *refs):
    s_refs = refs[:pieces]
    lt_ref, basis_ref, far_ref, sketch, gram4, padded = refs[pieces:]
    steps, height, kk, _ = s_refs[0].shape
    rows = 2 * steps * height
    sides = pieces // 2
    rank = kk * sides
    group = 256 // rank
    groups = rows // group
    batch = 8

    gram4[...] = jnp.zeros_like(gram4)
    pad_lags(lt_ref, padded)
    for j in range(steps):
        blocks = []
        for side in range(2):
            chunk = lax.rem((ids_ref[1] ^ side) - 2 * j + 2 * steps, 2 * steps)
            for i in range(height // group):
                block = jnp.concatenate(
                    [
                        s_refs[side * sides + q][j, group * i + x]
                        for x in range(group)
                        for q in range(sides)
                    ],
                    0,
                )
                start = pl.multiple_of(chunk * (height * rank) + 256 * i, 256)
                sketch[pl.ds(start, 256), :] = block
                blocks.append(block)
        wide = jnp.concatenate(blocks, 1)
        gram4[...] += matmul(wide, wide, NT)
    gram = sum(
        gram4[rank * i : rank * (i + 1), rank * i : rank * (i + 1)] for i in range(group)
    )
    coeffs = newton_schulz(gram)
    wide = jnp.concatenate([coeffs] * group, 1)
    wide = jnp.concatenate([wide] * group, 0)
    row = lax.broadcasted_iota(jnp.int32, (256, 256), 0) // rank
    col = lax.broadcasted_iota(jnp.int32, (256, 256), 1) // rank
    wide = jnp.where(row == col, wide, 0.0)
    both = jnp.concatenate(split(wide), 1)

    basis_ref[pl.ds(0, 2 * rank), :] = jnp.zeros((2 * rank, 128), BF16)
    basis_ref[pl.ds((rows + 2) * rank, 3 * rank), :] = jnp.zeros((3 * rank, 128), BF16)

    def rotate(s, carry):
        for k in range(batch // 2):
            first = pl.multiple_of((s * batch + 2 * k) * 256, 256)
            block = jnp.concatenate(
                [sketch[pl.ds(first, 256), :], sketch[pl.ds(first + 256, 256), :]], 1
            )
            value = matmul(both, jnp.concatenate([block, block], 0)).astype(BF16)
            basis_ref[pl.ds(first + 2 * rank, 256), :] = value[:, :128]
            basis_ref[pl.ds(first + 2 * rank + 256, 256), :] = value[:, 128:]
        return carry

    lax.fori_loop(0, groups // batch, rotate, 0)
    for e in range(far_ref.shape[0]):
        far_ref[e] = project_block(count, rank, e, ids_ref, basis_ref, padded)


def project(ids, sketches, lag_t, count):
    pieces = len(sketches)
    steps, height, kk, _ = sketches[0].shape
    rows = 2 * steps * height
    rank = kk * pieces // 2
    mm = 128 * 2 // pieces
    pairs = lag_t.shape[1] // mm
    return pl.pallas_call(
        functools.partial(project_kernel, count, pieces),
        out_shape=[
            jax.ShapeDtypeStruct(((rows + 5) * rank, 128), BF16),
            jax.ShapeDtypeStruct((count // 2, pairs, mm, 128), BF16),
        ],
        in_specs=[pl.BlockSpec(memory_space=pltpu.SMEM)]
        + [pl.BlockSpec(memory_space=pltpu.VMEM)] * (pieces + 1),
        out_specs=[pl.BlockSpec(memory_space=pltpu.VMEM)] * 2,
        scratch_shapes=[
            pltpu.VMEM((rows * rank, 128), BF16),
            pltpu.VMEM((256, 256), F32),
            pltpu.VMEM((2, 3 * pairs - 1, mm, 256), BF16),
        ],
        compiler_params=pltpu.CompilerParams(vmem_limit_bytes=VMEM_LIMIT),
        name="project",
    )(ids, *sketches, lag_t)


def project_rest(ids, basis, lag_t, count, rank):
    mm = 128 // (count - 1)
    pairs = lag_t.shape[1] // mm
    return pl.pallas_call(
        functools.partial(project_rest_kernel, count, rank),
        out_shape=[
            jax.ShapeDtypeStruct((count // 2, pairs, mm, 128), BF16),
            jax.ShapeDtypeStruct((pairs, mm, 128), BF16),
        ],
        in_specs=[pl.BlockSpec(memory_space=pltpu.SMEM)] + [pl.BlockSpec(memory_space=pltpu.VMEM)] * 2,
        out_specs=[pl.BlockSpec(memory_space=pltpu.VMEM)] * 2,
        scratch_shapes=[pltpu.VMEM((2, 3 * pairs - 1, mm, 256), BF16)],
        compiler_params=pltpu.CompilerParams(vmem_limit_bytes=VMEM_LIMIT),
        name="project_rest",
    )(ids, basis, lag_t)


def totals_kernel(count, halves, first, last, ids_ref, *refs):
    number = last - first + 1
    p_refs = refs[:number]
    final = first == 0
    if final:
        basis_ref, sums_ref, lt_ref, out_ref, wide, acc = refs[number:]
    else:
        basis_ref, acc, wide = refs[number:]
    pairs, mm, _ = p_refs[0].shape
    span = pairs * mm
    half = pairs // 2
    for x, h in enumerate(halves):
        wide[x, pl.ds(number * span - mm, mm), 128:] = jnp.zeros((mm, 128), BF16)
        acc[x] = sums_ref[h] if final else jnp.zeros((span, 256), F32)
    for e in range(number):
        block = p_refs[e][...].reshape(span, 128)
        zero = jnp.zeros_like(block)
        for x, h in enumerate(halves):
            kept = jnp.where(half_of(ids_ref, count, first + e) == h, block, zero)
            wide[x, pl.ds(e * span, span), :128] = kept
            if e == 0:
                wide[x, pl.ds(0, span - mm), 128:] = kept[mm:]
            else:
                wide[x, pl.ds(e * span - mm, span), 128:] = kept

    def chain(x, e, size):
        total = jnp.zeros((span, 256), F32)
        for k in range(size):
            start = pl.multiple_of((e * half + k) * 2 * mm, 32)
            tile = basis_tile(basis_ref, (first + e) * half + k, 64)
            total += matmul(wide[x, pl.ds(start, span), :], tile)
        acc[x] += total

    def step(e, carry):
        here, after = half_of(ids_ref, count, first + e), half_of(ids_ref, count, first + e + 1)
        for x, h in enumerate(halves):

            @pl.when(jnp.logical_or(here == h, after == h))
            def _():
                chain(x, e, half)

        return carry

    lax.fori_loop(0, last - first, step, 0)
    if not final:
        chain(0, last - first, 1)
        return
    blocks = 2 * pairs
    total_cols = blocks * lax.axis_size("col")
    b = lax.broadcasted_iota(jnp.int32, (pairs, 1, 256), 0)
    lane = lax.broadcasted_iota(jnp.int32, (pairs, 1, 256), 2)
    for h in halves:
        lag = h * total_cols + ids_ref[1] * blocks + 2 * b + lane // 128
        counts = lag_count(lag, blocks * (count - 1), total_cols)
        scaled = acc[h].reshape(pairs, mm, 256) * (1.0 / jnp.maximum(counts.astype(F32), 1.0))
        out_ref[h] = (scaled.reshape(span, 256) - SHARE * lt_ref[h].astype(F32)).astype(BF16)


def totals_near(ids, p_blocks, basis):
    count = len(p_blocks)
    first, last = count // 2, count - 1
    pairs, mm, _ = p_blocks[last].shape
    span = pairs * mm
    return pl.pallas_call(
        functools.partial(totals_kernel, count, (0, 1), first, last),
        out_shape=jax.ShapeDtypeStruct((2, span, 256), F32),
        in_specs=[pl.BlockSpec(memory_space=pltpu.SMEM)]
        + [pl.BlockSpec(memory_space=pltpu.VMEM)] * (last - first + 2),
        out_specs=pl.BlockSpec(memory_space=pltpu.VMEM),
        scratch_shapes=[pltpu.VMEM((2, (last - first + 1) * span, 256), BF16)],
        compiler_params=pltpu.CompilerParams(vmem_limit_bytes=VMEM_LIMIT),
        name="totals_near",
    )(ids, *p_blocks[first:], basis)


def totals_far(ids, p_blocks, basis, sums, lag_t):
    count = len(p_blocks)
    first, last = 0, count // 2
    pairs, mm, _ = p_blocks[first].shape
    span = pairs * mm
    return pl.pallas_call(
        functools.partial(totals_kernel, count, (0, 1), first, last),
        out_shape=jax.ShapeDtypeStruct((2, span, 256), BF16),
        in_specs=[pl.BlockSpec(memory_space=pltpu.SMEM)]
        + [pl.BlockSpec(memory_space=pltpu.VMEM)] * (last - first + 4),
        out_specs=pl.BlockSpec(memory_space=pltpu.VMEM),
        scratch_shapes=[
            pltpu.VMEM((2, (last - first + 1) * span, 256), BF16),
            pltpu.VMEM((2, span, 256), F32),
        ],
        compiler_params=pltpu.CompilerParams(vmem_limit_bytes=VMEM_LIMIT),
        name="totals_far",
    )(ids, *p_blocks[first : last + 1], basis, sums, lag_t)


def merge_kernel(offsets, total_rows, total_cols, ids_ref, *refs):
    count = len(offsets)
    d_refs, lag_ref, out_ref, square = refs[:count], refs[count], refs[count + 1], refs[count + 2]
    mm = 128 // count
    depth = square.shape[0]
    blocks = 2 * depth
    h = pl.program_id(0)
    row = lax.broadcasted_iota(jnp.int32, (128, 128), 0)
    col = lax.broadcasted_iota(jnp.int32, (128, 128), 1)
    eye = jnp.where(row == col, 1.0, 0.0).astype(BF16)
    for j in range(count):
        start = pl.multiple_of((ids_ref[0] ^ offsets[j]) * mm, mm)
        for b in range(depth):
            square[b, pl.ds(start, mm), :] = d_refs[j][0, pl.ds(b * mm, mm), :]
    for b in range(depth):
        for i in range(2):
            a = 2 * b + i
            full = lag_count(h * total_cols + ids_ref[1] * blocks + a, total_rows, total_cols) > 0
            keep = jnp.where(full, 0.5 + 0.5 * SHARE, 1.0)
            gain = jnp.where(full, 0.5, 0.0)
            turned = matmul(eye, square[b, :, 128 * i : 128 * (i + 1)], NT)
            out_ref[0, a] = keep * lag_ref[0, a].astype(F32) + gain * turned


def merge(ids, parts, offsets, markov, total_rows, total_cols):
    count = len(parts)
    halves, blocks, _, _ = markov.shape
    mm = 128 // count
    return pl.pallas_call(
        functools.partial(merge_kernel, tuple(offsets), total_rows, total_cols),
        out_shape=jax.ShapeDtypeStruct(markov.shape, F32),
        grid=(halves,),
        in_specs=[pl.BlockSpec(memory_space=pltpu.SMEM)]
        + [pl.BlockSpec((1, blocks // 2 * mm, 256), lambda h: (h, 0, 0))] * count
        + [pl.BlockSpec((1, blocks, 128, 128), lambda h: (h, 0, 0, 0))],
        out_specs=pl.BlockSpec((1, blocks, 128, 128), lambda h: (h, 0, 0, 0)),
        scratch_shapes=[pltpu.VMEM((blocks // 2, 128, 256), BF16)],
        compiler_params=pltpu.CompilerParams(vmem_limit_bytes=VMEM_LIMIT),
        name="merge",
    )(ids, *parts, markov)


def spread_rounds(count):
    rounds = [[(d, [0]) for d in (1, 2) if d < count]]
    have, shift = 3, 2
    while have < count:
        last = min(have + shift, count)
        rounds.append([(shift, list(range(have - shift, last - shift)))])
        have, shift = last, shift * 2
    return rounds


def spread_blocks(own, count, extra=None):
    got = {0: own}
    for number, step in enumerate(spread_rounds(count)):
        got.update({k + d: shift_col(got[k], d) for d, ks in step for k in ks})
        if extra is not None and number == 0:
            got, extra = lax.optimization_barrier((got, extra))
    return got, extra


def collect_blocks(far, middle, own, count):
    late = count // 2
    moved = shift_col(far, -late)
    middle = middle.astype(F32) + moved.astype(F32)
    total = {late - i: middle[i] for i in range(late)}
    total[0] = own.astype(F32)
    for step in reversed(spread_rounds(late + 1)):
        moved = [(k, shift_col(total[k + d].astype(BF16), -d)) for d, ks in step for k in ks]
        for k, block in moved:
            total[k] = total[k] + block.astype(F32)
    return total[0].astype(BF16)


def local(markov, omega):
    n_rows, n_cols = lax.axis_size("row"), lax.axis_size("col")
    r, c = lax.axis_index("row"), lax.axis_index("col")
    _, blocks, out_rows, columns = markov.shape
    rank = omega.shape[1]
    assert out_rows == 128 and columns == 128 and rank == 64 and n_rows >= 4
    kk, mm = rank // n_rows, columns // n_rows
    count = n_rows + 1
    pairs = blocks // 2
    rows = blocks * n_rows
    total_cols = blocks * n_cols
    distance = [count - 1 - e for e in range(count)]
    ids = jnp.stack([r, c]).astype(jnp.int32)

    own = omega.reshape(pairs, 2, columns, rank).transpose(0, 3, 1, 2).reshape(pairs, rank, 256)
    own = lax.dynamic_slice_in_dim(own, r * kk, kk, 1)
    lag_t = lax.dynamic_slice_in_dim(markov, r * mm, mm, 3)
    lag_t = lag_t.reshape(2, pairs, 2, out_rows, mm).transpose(0, 1, 4, 2, 3).reshape(2, pairs * mm, 256)
    got, lag_t = spread_blocks(own, count, lag_t)
    w_blocks = [got[d] for d in distance]

    late = count // 2
    partial = sketch_part(ids, markov, w_blocks, late, count - 1, rows)
    partial = sketch_part(ids, markov, w_blocks, 0, late, rows, partial)
    partial = lax.all_to_all(partial, "col", 0, 0, tiled=True)
    chunk = partial.reshape(n_cols, rows // n_cols, kk, 128).astype(F32).sum(0).astype(BF16)
    even = jnp.stack([chunk] + [shift_col(chunk, d) for d in range(2, n_cols, 2)])
    odd = swap("col", even, 1)
    sketches = gather_row(even)[0] + gather_row(odd)[0]

    basis, far = project(ids, sketches, lag_t, count)
    middle, mine = project_rest(ids, basis, lag_t, count, rank)
    mine = collect_blocks(far, middle, mine, count)
    got, _ = spread_blocks(mine, count)
    p_blocks = [got[d] for d in distance]

    sums = totals_near(ids, p_blocks, basis)
    part = totals_far(ids, p_blocks, basis, sums, lag_t)
    parts, offsets = gather_row(part)
    return merge(ids, parts, offsets, markov, rows, total_cols)


def solution(mesh):
    in_specs = (P(None, "col", None, None), P("col", None))
    out_specs = P(None, "col", None, None)
    return jax.shard_map(local, mesh=mesh, in_specs=in_specs, out_specs=out_specs, check_vma=False)
```

time: 157 us -> 140 us (0.89)
  blocking collectives: 34 us -> 16.7 us
  waiting for transfers between devices: 56.5 us -> 42.5 us
  Pallas kernels: 33.2 us -> 42.1 us
  starting transfers between devices: 17.3 us -> 24 us
    all_to_all x1 -> x0, blocking collectives: 17.5 us -> none  [local(): lax.all_to_all(spread, 'col', 0, 0, tiled=True).reshape(rows, kk, 128)]
    pallas_call x3 -> x6, Pallas kernels: 19.4 us -> 31.4 us  [the longest x2 10.5 us: sketch_part(): pl.pallas_call(functools.partial(sketch_kernel, count, first, last), out_...]
    ppermute x12 -> x14, waiting for transfers between devices: 33.8 us -> 22.7 us  [shift_col(): return lax.ppermute(x, 'col', [(i, (i + distance) % n) for i in range(n)])]
    ppermute x12 -> x14, starting transfers between devices: 14.3 us -> 18.1 us  [shift_col(): return lax.ppermute(x, 'col', [(i, (i + distance) % n) for i in range(n)])]
    pallas_call x1, Pallas kernels: 13.8 us -> 10.7 us  [project(): pl.pallas_call(functools.partial(project_kernel, count, pieces), out_shap...]
    ppermute x6 -> x10, starting transfers between devices: 2.99 us -> 5.89 us  [swap(): return lax.ppermute(x, axis, [(i, i ^ bit) for i in range(n)])]
    ppermute x6 -> x10, waiting for transfers between devices: 22.7 us -> 19.8 us  [swap(): return lax.ppermute(x, axis, [(i, i ^ bit) for i in range(n)])]
    convert_element_type x2 -> x0, other arithmetic: 1.88 us -> none  [collect_blocks(): total[k + d].astype(BF16)]
  transfers between devices with their start and end apart: 18 -> 24, of which waited for: 13 -> 17; matrix products, arithmetic and copies ran while one was open for 5% -> 5% of each run, Pallas kernels for 0% -> 12%
where the time goes in v3:
time: 140 us
  waiting for transfers between devices  42.5 us (30%)
  Pallas kernels  42.1 us (30%)
  starting transfers between devices  24 us (17%)
  blocking collectives  16.7 us (12%)
  local copies, waits for them, and re-layouts  11.4 us (8%)
  other arithmetic  2.75 us (2%)
    ppermute x14, waiting for transfers between devices, shift_col(): return lax.ppermute(x, 'col', [(i, (i + distance) % n) for i in range(n)])  22.7 us
    ppermute x10, waiting for transfers between devices, swap(): return lax.ppermute(x, axis, [(i, i ^ bit) for i in range(n)])  19.8 us
    ppermute x14, starting transfers between devices, shift_col(): return lax.ppermute(x, 'col', [(i, (i + distance) % n) for i in range(n)])  18.1 us
    all_to_all x1, blocking collectives, local(): partial = lax.all_to_all(partial, 'col', 0, 0, tiled=True)  16.7 us
    pallas_call x1, Pallas kernels, project(): pl.pallas_call(functools.partial(project_kernel, count, pieces), out_shap...  10.7 us
    pallas_call x2, Pallas kernels, sketch_part(): pl.pallas_call(functools.partial(sketch_kernel, count, first, last), out_...  10.5 us
    ppermute x10, starting transfers between devices, swap(): return lax.ppermute(x, axis, [(i, i ^ bit) for i in range(n)])  5.89 us
    pallas_call x1, Pallas kernels, project_rest(): pl.pallas_call(functools.partial(project_rest_kernel, count, rank), out_s...  5.62 us
  transfers between devices with their start and end apart: 24, of which 17 were waited for; matrix products, arithmetic and copies ran while one was open for 5% of the time, Pallas kernels for 12%

profile of v3, /device:TPU:0, one launch (start us, length us, event | category | flops | bytes accessed | tf_op | source)
XLA Modules:
  0.0 139.7 jit_solution(3861248696201294787)
XLA Ops:
  0.0 1.6 %reshape.17 = bf16[16,2,128,64]{2,1,0,3:T(2,128)(2,1)S(1)} reshape(bf16[4096,64]{0,1:T(8,128)(2,1)} %param.3) | data formatting | bytes 1048576 | tf_op jit(solution)/shard_map/reshape | solution.py:497
  2.4 3.1 %collective-permute-start.1 = (bf16[16,16,256]{2,1,0:T(8,128)(2,1)S(1)}, bf16[16,16,256]{2,1,0:T(8,128)(2,1)S(1)}, u32[]{:S(2)}, u32[]{:S(2)}) collective-permute-start(bf16[16,16,256]{2,1,0:T(8,128)(2,1)S(1)} %constant_dynamic-slice_fusion.1.refs_2_), channel_id=1, source_target_pairs={{0,2},{1,3},{2,4},{3,5},{4,6},{5,7},{6,0},{7,1},{8,10},{9,11},{10,... | collective-permute-start | bytes 393224 | tf_op jit(solution)/shard_map/ppermute | solution.py:29
  7.1 2.0 %constant_dynamic-slice_fusion = bf16[2,32,128,32]{3,2,1,0:T(8,128)(2,1)} fusion(bf16[2,32,128,128]{3,2,1,0:T(8,128)(2,1)S(1)} %copy-done, s32[]{:T(128)S(6)} %select_n.7), kind=kLoop, calls=%fused_computation.7 | loop fusion | bytes 1048580 | tf_op jit(solution)/shard_map/dynamic_slice | solution.py:499
  9.0 3.0 %copy.7 = bf16[2,16,32,2,128]{4,3,2,1,0:T(2,128)(2,1)S(1)} copy(bf16[2,16,32,2,128]{2,4,3,1,0:T(8,128)(2,1)} %bitcast.20) | data formatting | bytes 1048576 | tf_op jit(solution)/shard_map/transpose | solution.py:500
  13.2 1.6 %collective-permute-done.refs_1_ = bf16[16,16,256]{2,1,0:T(8,128)(2,1)S(1)} collective-permute-done((bf16[16,16,256]{2,1,0:T(8,128)(2,1)S(1)}, bf16[16,16,256]{2,1,0:T(8,128)(2,1)S(1)}, u32[]{:S(2)}, u32[]{:S(2)}) %collective-permute-start) | collective-permute-done | bytes 131104 | tf_op jit(solution)/shard_map/ppermute | solution.py:29
  14.8 1.6 %collective-permute-start.2 = (bf16[16,16,256]{2,1,0:T(8,128)(2,1)S(1)}, bf16[16,16,256]{2,1,0:T(8,128)(2,1)S(1)}, u32[]{:S(2)}, u32[]{:S(2)}) collective-permute-start(bf16[16,16,256]{2,1,0:T(8,128)(2,1)S(1)} %collective-permute-done.1.refs_0_.refs_2_), channel_id=1, source_target_pairs={{0,2},{1,3},{2,4},{3,5},{4,6},{5,7},{6,0},{7,1},{8,10},{9,11},{10,... | collective-permute-start | bytes 393224 | tf_op jit(solution)/shard_map/ppermute | solution.py:29
  17.1 5.5 %sketch.2.refs_3_ = bf16[128,16,128]{2,1,0:T(8,128)(2,1)} custom-call(s32[2]{0:T(128)} %pad_add_fusion.ids_ref, bf16[2,32,128,128]{3,2,1,0:T(8,128)(2,1)} %refs_4_.1, bf16[16,16,256]{2,1,0:T(8,128)(2,1)} %copy-done.8, bf16[16,16,256]{2,1,0:T(8,128)(2,1)} %copy-done.16, bf16[16,16,256]{2,1,0:T(8,128)(2,1)} %copy-done.6), custom_call_target="tpu_custom_call" | custom-call | tf_op jit(solution)/shard_map/sketch/pallas_call | solution.py:127
  24.5 4.9 %sketch.3 = bf16[128,16,128]{2,1,0:T(8,128)(2,1)} custom-call(s32[2]{0:T(128)} %pad_add_fusion.ids_ref, bf16[2,32,128,128]{3,2,1,0:T(8,128)(2,1)} %refs_4_.1, bf16[16,16,256]{2,1,0:T(8,128)(2,1)} %copy-done.21, bf16[16,16,256]{2,1,0:T(8,128)(2,1)} %copy-done.20, bf16[16,16,256]{2,1,0:T(8,128)(2,1)} %copy-done.8, ...), custom_call_target="tpu_custom_call", output_to_operand_aliasing={{}: (5, {})} | custom-call | tf_op jit(solution)/shard_map/sketch/pallas_call | solution.py:127
  29.5 16.7 %all_to_all.5 = bf16[128,16,128]{2,1,0:T(8,128)(2,1)S(1)} all-to-all(bf16[128,16,128]{2,1,0:T(8,128)(2,1)} %sketch.3), channel_id=1, replica_groups=mesh['row'=4,'col'=8] {'col'}, dimensions={0} | all-to-all | bytes 1048576 | tf_op jit(solution)/shard_map/all_to_all | solution.py:507
  49.4 2.0 %collective-permute-done.6 = bf16[16,16,128]{2,1,0:T(8,128)(2,1)S(1)} collective-permute-done((bf16[16,16,128]{2,1,0:T(8,128)(2,1)S(1)}, bf16[16,16,128]{2,1,0:T(8,128)(2,1)S(1)}, u32[]{:S(2)}, u32[]{:S(2)}) %collective-permute-start.6) | collective-permute-done | bytes 65568 | tf_op jit(solution)/shard_map/ppermute | solution.py:29
  51.4 2.2 %collective-permute-done.5 = bf16[16,16,128]{2,1,0:T(8,128)(2,1)S(1)} collective-permute-done((bf16[16,16,128]{2,1,0:T(8,128)(2,1)S(1)}, bf16[16,16,128]{2,1,0:T(8,128)(2,1)S(1)}, u32[]{:S(2)}, u32[]{:S(2)}) %collective-permute-start.5) | collective-permute-done | bytes 65568 | tf_op jit(solution)/shard_map/ppermute | solution.py:29
  57.4 4.0 %collective-permute-done.10.refs_4_ = bf16[4,16,16,128]{3,2,1,0:T(8,128)(2,1)S(1)} collective-permute-done((bf16[4,16,16,128]{3,2,1,0:T(8,128)(2,1)S(1)}, bf16[4,16,16,128]{3,2,1,0:T(8,128)(2,1)S(1)}, u32[]{:S(2)}, u32[]{:S(2)}) %collective-permute-start.10) | collective-permute-done | bytes 262176 | tf_op jit(solution)/shard_map/ppermute | solution.py:34
  64.7 3.1 %collective-permute-done.11.refs_5_ = bf16[4,16,16,128]{3,2,1,0:T(8,128)(2,1)S(1)} collective-permute-done((bf16[4,16,16,128]{3,2,1,0:T(8,128)(2,1)S(1)}, bf16[4,16,16,128]{3,2,1,0:T(8,128)(2,1)S(1)}, u32[]{:S(2)}, u32[]{:S(2)}) %collective-permute-start.11) | collective-permute-done | bytes 262176 | tf_op jit(solution)/shard_map/ppermute | solution.py:34
  70.2 10.7 %project.1 = (bf16[8512,128]{1,0:T(8,128)(2,1)}, bf16[2,16,32,128]{3,2,1,0:T(8,128)(2,1)}) custom-call(s32[2]{0:T(128)} %pad_add_fusion.ids_ref, bf16[4,16,16,128]{3,2,1,0:T(8,128)(2,1)} %copy-done.1, bf16[4,16,16,128]{3,2,1,0:T(8,128)(2,1)} %copy-done.10, bf16[4,16,16,128]{3,2,1,0:T(8,128)(2,1)} %copy-done.12, bf16[4,16,16,128]{3,2,1,0:T(8,128)(2,1)} %copy-done.14, ...), custom_call_target="tpu_custom_call" | custom-call | tf_op jit(solution)/shard_map/project/pallas_call | solution.py:278
  82.3 5.6 %project_rest.1 = (bf16[2,16,32,128]{3,2,1,0:T(8,128)(2,1)}, bf16[16,32,128]{2,1,0:T(8,128)(2,1)}) custom-call(s32[2]{0:T(128)} %pad_add_fusion.ids_ref, bf16[8512,128]{1,0:T(8,128)(2,1)} %get-tuple-element.17.basis_ref.refs_3_, bf16[2,512,256]{2,1,0:T(8,128)(2,1)} %reshape.20.refs_8_.lt_ref.refs_5_), custom_call_target="tpu_custom_call" | custom-call | tf_op jit(solution)/shard_map/project_rest/pallas_call | solution.py:300
  87.9 1.6 %collective-permute-done.14 = bf16[2,16,32,128]{3,2,1,0:T(8,128)(2,1)S(1)} collective-permute-done((bf16[2,16,32,128]{3,2,1,0:T(8,128)(2,1)}, bf16[2,16,32,128]{3,2,1,0:T(8,128)(2,1)S(1)}, u32[]{:S(2)}, u32[]{:S(2)}) %collective-permute-start.14) | collective-permute-done | bytes 262176 | tf_op jit(solution)/shard_map/ppermute | solution.py:29
  90.5 3.4 %collective-permute-start.15 = (bf16[16,32,128]{2,1,0:T(8,128)(2,1)S(1)}, bf16[16,32,128]{2,1,0:T(8,128)(2,1)S(1)}, u32[]{:S(2)}, u32[]{:S(2)}) collective-permute-start(bf16[16,32,128]{2,1,0:T(8,128)(2,1)S(1)} %get-tuple-element.21), channel_id=1, source_target_pairs={{0,7},{1,0},{2,1},{3,2},{4,3},{5,4},{6,5},{7,6},{8,15},{9,8},{10,9... | collective-permute-start | bytes 393224 | tf_op jit(solution)/shard_map/ppermute | solution.py:29
  95.2 2.3 %collective-permute-done.15 = bf16[16,32,128]{2,1,0:T(8,128)(2,1)S(1)} collective-permute-done((bf16[16,32,128]{2,1,0:T(8,128)(2,1)S(1)}, bf16[16,32,128]{2,1,0:T(8,128)(2,1)S(1)}, u32[]{:S(2)}, u32[]{:S(2)}) %collective-permute-start.15) | collective-permute-done | bytes 131104 | tf_op jit(solution)/shard_map/ppermute | solution.py:29
  101.4 7.6 %collective-permute-done.19.refs_1_ = bf16[16,32,128]{2,1,0:T(8,128)(2,1)S(1)} collective-permute-done((bf16[16,32,128]{2,1,0:T(8,128)(2,1)S(1)}, bf16[16,32,128]{2,1,0:T(8,128)(2,1)S(1)}, u32[]{:S(2)}, u32[]{:S(2)}) %collective-permute-start.19) | collective-permute-done | bytes 131104 | tf_op jit(solution)/shard_map/ppermute | solution.py:29
  110.1 5.5 %totals_near.1.refs_4_ = f32[2,512,256]{2,1,0:T(8,128)} custom-call(s32[2]{0:T(128)} %pad_add_fusion.ids_ref, bf16[16,32,128]{2,1,0:T(8,128)(2,1)} %copy-done.5, bf16[16,32,128]{2,1,0:T(8,128)(2,1)} %copy-done.17, bf16[16,32,128]{2,1,0:T(8,128)(2,1)} %copy-done.7, bf16[8512,128]{1,0:T(8,128)(2,1)} %get-tuple-element.17.basis_ref.refs_3_), custom_call_target="tpu_custom_call" | custom-call | tf_op jit(solution)/shard_map/totals_near/pallas_call | solution.py:377
  117.8 5.0 %totals_far.1.refs_0_ = bf16[2,512,256]{2,1,0:T(8,128)(2,1)} custom-call(s32[2]{0:T(128)} %pad_add_fusion.ids_ref, bf16[16,32,128]{2,1,0:T(8,128)(2,1)} %copy-done.19, bf16[16,32,128]{2,1,0:T(8,128)(2,1)} %copy-done.18, bf16[16,32,128]{2,1,0:T(8,128)(2,1)} %copy-done.5, bf16[8512,128]{1,0:T(8,128)(2,1)} %get-tuple-element.17.basis_ref.refs_3_, ...), custom_call_target="tpu_custom_call" | custom-call | tf_op jit(solution)/shard_map/totals_far/pallas_call | solution.py:394
  124.3 7.9 %collective-permute-done.21.refs_1_ = bf16[2,512,256]{2,1,0:T(8,128)(2,1)S(1)} collective-permute-done((bf16[2,512,256]{2,1,0:T(8,128)(2,1)}, bf16[2,512,256]{2,1,0:T(8,128)(2,1)S(1)}, u32[]{:S(2)}, u32[]{:S(2)}) %collective-permute-start.21) | collective-permute-done | bytes 524320 | tf_op jit(solution)/shard_map/ppermute | solution.py:34
  132.2 1.9 %collective-permute-done.23.refs_3_ = bf16[2,512,256]{2,1,0:T(8,128)(2,1)S(1)} collective-permute-done((bf16[2,512,256]{2,1,0:T(8,128)(2,1)S(1)}, bf16[2,512,256]{2,1,0:T(8,128)(2,1)S(1)}, u32[]{:S(2)}, u32[]{:S(2)}) %collective-permute-start.23) | collective-permute-done | bytes 524320 | tf_op jit(solution)/shard_map/ppermute | solution.py:34
  134.9 4.8 %merge.1 = f32[2,32,128,128]{3,2,1,0:T(8,128)} custom-call(s32[2]{0:T(128)} %pad_add_fusion.ids_ref, bf16[2,512,256]{2,1,0:T(8,128)(2,1)} %totals_far.1.refs_0_, bf16[2,512,256]{2,1,0:T(8,128)(2,1)} %copy-done.2, bf16[2,512,256]{2,1,0:T(8,128)(2,1)} %copy-done.3, bf16[2,512,256]{2,1,0:T(8,128)(2,1)} %copy-done.4, bf16[2,32,128,128]{3,2,1,0:T(8,128)(2,1)} %refs_4_.1), custom_call_target="tpu_custom_call" | custom-call | tf_op jit(solution)/shard_map/merge/pallas_call | solution.py:437
  (89 shorter events, 31.7 us)
Async XLA Ops:
  2.4 10.8 %collective-permute-start.1 = (bf16[16,16,256]{2,1,0:T(8,128)(2,1)S(1)}, bf16[16,16,256]{2,1,0:T(8,128)(2,1)S(1)}, u32[]{:S(2)}, u32[]{:S(2)}) collective-permute-start(bf16[16,16,256]{2,1,0:T(8,128)(2,1)S(1)} %constant_dynamic-slice_fusion.1.refs_2_), channel_id=1, source_target_pairs={{0,2},{1,3},{2,4},{3,5},{4,6},{5,7},{6,0},{7,1},{8,10},{9,11},{10,... | collective-permute-start | bytes 393224 | tf_op jit(solution)/shard_map/ppermute | solution.py:29
  5.5 9.3 %collective-permute-start = (bf16[16,16,256]{2,1,0:T(8,128)(2,1)S(1)}, bf16[16,16,256]{2,1,0:T(8,128)(2,1)S(1)}, u32[]{:S(2)}, u32[]{:S(2)}) collective-permute-start(bf16[16,16,256]{2,1,0:T(8,128)(2,1)S(1)} %constant_dynamic-slice_fusion.1.refs_2_), channel_id=1, source_target_pairs={{0,1},{1,2},{2,3},{3,4},{4,5},{5,6},{6,7},{7,0},{8,9},{9,10},{10,1... | collective-permute-start | bytes 393224 | tf_op jit(solution)/shard_map/ppermute | solution.py:29
  14.8 7.8 %collective-permute-start.3 = (bf16[16,16,256]{2,1,0:T(8,128)(2,1)S(1)}, bf16[16,16,256]{2,1,0:T(8,128)(2,1)S(1)}, u32[]{:S(2)}, u32[]{:S(2)}) collective-permute-start(bf16[16,16,256]{2,1,0:T(8,128)(2,1)S(1)} %collective-permute-done.refs_1_), channel_id=1, source_target_pairs={{0,2},{1,3},{2,4},{3,5},{4,6},{5,7},{6,0},{7,1},{8,10},{9,11},{10,... | collective-permute-start | bytes 393224 | tf_op jit(solution)/shard_map/ppermute | solution.py:29
  14.8 9.0 %collective-permute-start.2 = (bf16[16,16,256]{2,1,0:T(8,128)(2,1)S(1)}, bf16[16,16,256]{2,1,0:T(8,128)(2,1)S(1)}, u32[]{:S(2)}, u32[]{:S(2)}) collective-permute-start(bf16[16,16,256]{2,1,0:T(8,128)(2,1)S(1)} %collective-permute-done.1.refs_0_.refs_2_), channel_id=1, source_target_pairs={{0,2},{1,3},{2,4},{3,5},{4,6},{5,7},{6,0},{7,1},{8,10},{9,11},{10,... | collective-permute-start | bytes 393224 | tf_op jit(solution)/shard_map/ppermute | solution.py:29
  46.2 5.2 %collective-permute-start.6 = (bf16[16,16,128]{2,1,0:T(8,128)(2,1)S(1)}, bf16[16,16,128]{2,1,0:T(8,128)(2,1)S(1)}, u32[]{:S(2)}, u32[]{:S(2)}) collective-permute-start(bf16[16,16,128]{2,1,0:T(8,128)(2,1)S(1)} %reduce_sum.12), channel_id=1, source_target_pairs={{0,6},{1,7},{2,0},{3,1},{4,2},{5,3},{6,4},{7,5},{8,14},{9,15},{10,... | collective-permute-start | bytes 196616 | tf_op jit(solution)/shard_map/ppermute | solution.py:29
  47.5 6.2 %collective-permute-start.5 = (bf16[16,16,128]{2,1,0:T(8,128)(2,1)S(1)}, bf16[16,16,128]{2,1,0:T(8,128)(2,1)S(1)}, u32[]{:S(2)}, u32[]{:S(2)}) collective-permute-start(bf16[16,16,128]{2,1,0:T(8,128)(2,1)S(1)} %reduce_sum.12), channel_id=1, source_target_pairs={{0,4},{1,5},{2,6},{3,7},{4,0},{5,1},{6,2},{7,3},{8,12},{9,13},{10,... | collective-permute-start | bytes 196616 | tf_op jit(solution)/shard_map/ppermute | solution.py:29
  48.8 6.1 %collective-permute-start.4 = (bf16[16,16,128]{2,1,0:T(8,128)(2,1)S(1)}, bf16[16,16,128]{2,1,0:T(8,128)(2,1)S(1)}, u32[]{:S(2)}, u32[]{:S(2)}) collective-permute-start(bf16[16,16,128]{2,1,0:T(8,128)(2,1)S(1)} %reduce_sum.12), channel_id=1, source_target_pairs={{0,2},{1,3},{2,4},{3,5},{4,6},{5,7},{6,0},{7,1},{8,10},{9,11},{10,... | collective-permute-start | bytes 196616 | tf_op jit(solution)/shard_map/ppermute | solution.py:29
  55.0 6.4 %collective-permute-start.10 = (bf16[4,16,16,128]{3,2,1,0:T(8,128)(2,1)S(1)}, bf16[4,16,16,128]{3,2,1,0:T(8,128)(2,1)S(1)}, u32[]{:S(2)}, u32[]{:S(2)}) collective-permute-start(bf16[4,16,16,128]{3,2,1,0:T(8,128)(2,1)S(1)} %pad_maximum_fusion.refs_0_), channel_id=1, source_target_pairs={{0,1},{1,0},{2,3},{3,2},{4,5},{5,4},{6,7},{7,6},{8,9},{9,8},{10,11... | collective-permute-start | bytes 786440 | tf_op jit(solution)/shard_map/ppermute | solution.py:34
  55.9 8.8 %collective-permute-start.7 = (bf16[4,16,16,128]{3,2,1,0:T(8,128)(2,1)S(1)}, bf16[4,16,16,128]{3,2,1,0:T(8,128)(2,1)S(1)}, u32[]{:S(2)}, u32[]{:S(2)}) collective-permute-start(bf16[4,16,16,128]{3,2,1,0:T(8,128)(2,1)S(1)} %pad_maximum_fusion.refs_0_), channel_id=1, source_target_pairs={{0,16},{8,24},{16,0},{24,8},{1,17},{9,25},{17,1},{25,9},{2,18},{10... | collective-permute-start | bytes 786440 | tf_op jit(solution)/shard_map/ppermute | solution.py:34
  61.4 6.5 %collective-permute-start.11 = (bf16[4,16,16,128]{3,2,1,0:T(8,128)(2,1)S(1)}, bf16[4,16,16,128]{3,2,1,0:T(8,128)(2,1)S(1)}, u32[]{:S(2)}, u32[]{:S(2)}) collective-permute-start(bf16[4,16,16,128]{3,2,1,0:T(8,128)(2,1)S(1)} %collective-permute-done.10.refs_4_), channel_id=1, source_target_pairs={{0,16},{8,24},{16,0},{24,8},{1,17},{9,25},{17,1},{25,9},{2,18},{10... | collective-permute-start | bytes 786440 | tf_op jit(solution)/shard_map/ppermute | solution.py:34
  62.9 5.0 %collective-permute-start.8 = (bf16[4,16,16,128]{3,2,1,0:T(8,128)(2,1)S(1)}, bf16[4,16,16,128]{3,2,1,0:T(8,128)(2,1)S(1)}, u32[]{:S(2)}, u32[]{:S(2)}) collective-permute-start(bf16[4,16,16,128]{3,2,1,0:T(8,128)(2,1)S(1)} %pad_maximum_fusion.refs_0_), channel_id=1, source_target_pairs={{0,8},{8,0},{16,24},{24,16},{1,9},{9,1},{17,25},{25,17},{2,10},{10... | collective-permute-start | bytes 786440 | tf_op jit(solution)/shard_map/ppermute | solution.py:34
  62.9 5.0 %collective-permute-start.12 = (bf16[4,16,16,128]{3,2,1,0:T(8,128)(2,1)S(1)}, bf16[4,16,16,128]{3,2,1,0:T(8,128)(2,1)S(1)}, u32[]{:S(2)}, u32[]{:S(2)}) collective-permute-start(bf16[4,16,16,128]{3,2,1,0:T(8,128)(2,1)S(1)} %collective-permute-done.10.refs_4_), channel_id=1, source_target_pairs={{0,8},{8,0},{16,24},{24,16},{1,9},{9,1},{17,25},{25,17},{2,10},{10... | collective-permute-start | bytes 786440 | tf_op jit(solution)/shard_map/ppermute | solution.py:34
  64.7 3.2 %collective-permute-start.9 = (bf16[4,16,16,128]{3,2,1,0:T(8,128)(2,1)S(1)}, bf16[4,16,16,128]{3,2,1,0:T(8,128)(2,1)S(1)}, u32[]{:S(2)}, u32[]{:S(2)}) collective-permute-start(bf16[4,16,16,128]{3,2,1,0:T(8,128)(2,1)S(1)} %collective-permute-done.7.refs_1_), channel_id=1, source_target_pairs={{0,8},{8,0},{16,24},{24,16},{1,9},{9,1},{17,25},{25,17},{2,10},{10... | collective-permute-start | bytes 786440 | tf_op jit(solution)/shard_map/ppermute | solution.py:34
  67.9 1.5 %collective-permute-start.13 = (bf16[4,16,16,128]{3,2,1,0:T(8,128)(2,1)S(1)}, bf16[4,16,16,128]{3,2,1,0:T(8,128)(2,1)S(1)}, u32[]{:S(2)}, u32[]{:S(2)}) collective-permute-start(bf16[4,16,16,128]{3,2,1,0:T(8,128)(2,1)S(1)} %collective-permute-done.11.refs_5_), channel_id=1, source_target_pairs={{0,8},{8,0},{16,24},{24,16},{1,9},{9,1},{17,25},{25,17},{2,10},{10... | collective-permute-start | bytes 786440 | tf_op jit(solution)/shard_map/ppermute | solution.py:34
  80.9 8.6 %collective-permute-start.14 = (bf16[2,16,32,128]{3,2,1,0:T(8,128)(2,1)}, bf16[2,16,32,128]{3,2,1,0:T(8,128)(2,1)S(1)}, u32[]{:S(2)}, u32[]{:S(2)}) collective-permute-start(bf16[2,16,32,128]{3,2,1,0:T(8,128)(2,1)} %get-tuple-element.20), channel_id=1, source_target_pairs={{0,6},{1,7},{2,0},{3,1},{4,2},{5,3},{6,4},{7,5},{8,14},{9,15},{10,... | collective-permute-start | bytes 786440 | tf_op jit(solution)/shard_map/ppermute | solution.py:29
  90.5 7.0 %collective-permute-start.15 = (bf16[16,32,128]{2,1,0:T(8,128)(2,1)S(1)}, bf16[16,32,128]{2,1,0:T(8,128)(2,1)S(1)}, u32[]{:S(2)}, u32[]{:S(2)}) collective-permute-start(bf16[16,32,128]{2,1,0:T(8,128)(2,1)S(1)} %get-tuple-element.21), channel_id=1, source_target_pairs={{0,7},{1,0},{2,1},{3,2},{4,3},{5,4},{6,5},{7,6},{8,15},{9,8},{10,9... | collective-permute-start | bytes 393224 | tf_op jit(solution)/shard_map/ppermute | solution.py:29
  93.9 5.0 %collective-permute-start.16 = (bf16[16,32,128]{2,1,0:T(8,128)(2,1)S(1)}, bf16[16,32,128]{2,1,0:T(8,128)(2,1)S(1)}, u32[]{:S(2)}, u32[]{:S(2)}) collective-permute-start(bf16[16,32,128]{2,1,0:T(8,128)(2,1)S(1)} %get-tuple-element.22), channel_id=1, source_target_pairs={{0,6},{1,7},{2,0},{3,1},{4,2},{5,3},{6,4},{7,5},{8,14},{9,15},{10,... | collective-permute-start | bytes 393224 | tf_op jit(solution)/shard_map/ppermute | solution.py:29
  99.9 9.1 %collective-permute-start.19 = (bf16[16,32,128]{2,1,0:T(8,128)(2,1)S(1)}, bf16[16,32,128]{2,1,0:T(8,128)(2,1)S(1)}, u32[]{:S(2)}, u32[]{:S(2)}) collective-permute-start(bf16[16,32,128]{2,1,0:T(8,128)(2,1)S(1)} %add_convert_fusion.1.refs_2_), channel_id=1, source_target_pairs={{0,1},{1,2},{2,3},{3,4},{4,5},{5,6},{6,7},{7,0},{8,9},{9,10},{10,1... | collective-permute-start | bytes 393224 | tf_op jit(solution)/shard_map/ppermute | solution.py:29
  100.0 9.1 %collective-permute-start.17 = (bf16[16,32,128]{2,1,0:T(8,128)(2,1)S(1)}, bf16[16,32,128]{2,1,0:T(8,128)(2,1)S(1)}, u32[]{:S(2)}, u32[]{:S(2)}) collective-permute-start(bf16[16,32,128]{2,1,0:T(8,128)(2,1)S(1)} %add_convert_fusion.1.refs_2_), channel_id=1, source_target_pairs={{0,2},{1,3},{2,4},{3,5},{4,6},{5,7},{6,0},{7,1},{8,10},{9,11},{10,... | collective-permute-start | bytes 393224 | tf_op jit(solution)/shard_map/ppermute | solution.py:29
  109.0 6.8 %collective-permute-start.20 = (bf16[16,32,128]{2,1,0:T(8,128)(2,1)S(1)}, bf16[16,32,128]{2,1,0:T(8,128)(2,1)S(1)}, u32[]{:S(2)}, u32[]{:S(2)}) collective-permute-start(bf16[16,32,128]{2,1,0:T(8,128)(2,1)S(1)} %collective-permute-done.19.refs_1_), channel_id=1, source_target_pairs={{0,2},{1,3},{2,4},{3,5},{4,6},{5,7},{6,0},{7,1},{8,10},{9,11},{10,... | collective-permute-start | bytes 393224 | tf_op jit(solution)/shard_map/ppermute | solution.py:29
  109.0 8.2 %collective-permute-start.18 = (bf16[16,32,128]{2,1,0:T(8,128)(2,1)S(1)}, bf16[16,32,128]{2,1,0:T(8,128)(2,1)S(1)}, u32[]{:S(2)}, u32[]{:S(2)}) collective-permute-start(bf16[16,32,128]{2,1,0:T(8,128)(2,1)S(1)} %collective-permute-done.17.refs_0_.refs_2_), channel_id=1, source_target_pairs={{0,2},{1,3},{2,4},{3,5},{4,6},{5,7},{6,0},{7,1},{8,10},{9,11},{10,... | collective-permute-start | bytes 393224 | tf_op jit(solution)/shard_map/ppermute | solution.py:29
  122.8 9.4 %collective-permute-start.21 = (bf16[2,512,256]{2,1,0:T(8,128)(2,1)}, bf16[2,512,256]{2,1,0:T(8,128)(2,1)S(1)}, u32[]{:S(2)}, u32[]{:S(2)}) collective-permute-start(bf16[2,512,256]{2,1,0:T(8,128)(2,1)} %totals_far.1.refs_0_), channel_id=1, source_target_pairs={{0,16},{8,24},{16,0},{24,8},{1,17},{9,25},{17,1},{25,9},{2,18},{10... | collective-permute-start | bytes 1572872 | tf_op jit(solution)/shard_map/ppermute | solution.py:34
  124.3 7.9 %collective-permute-start.22 = (bf16[2,512,256]{2,1,0:T(8,128)(2,1)}, bf16[2,512,256]{2,1,0:T(8,128)(2,1)S(1)}, u32[]{:S(2)}, u32[]{:S(2)}) collective-permute-start(bf16[2,512,256]{2,1,0:T(8,128)(2,1)} %totals_far.1.refs_0_), channel_id=1, source_target_pairs={{0,8},{8,0},{16,24},{24,16},{1,9},{9,1},{17,25},{25,17},{2,10},{10... | collective-permute-start | bytes 1572872 | tf_op jit(solution)/shard_map/ppermute | solution.py:34
  132.2 1.9 %collective-permute-start.23 = (bf16[2,512,256]{2,1,0:T(8,128)(2,1)S(1)}, bf16[2,512,256]{2,1,0:T(8,128)(2,1)S(1)}, u32[]{:S(2)}, u32[]{:S(2)}) collective-permute-start(bf16[2,512,256]{2,1,0:T(8,128)(2,1)S(1)} %collective-permute-done.21.refs_1_), channel_id=1, source_target_pairs={{0,8},{8,0},{16,24},{24,16},{1,9},{9,1},{17,25},{25,17},{2,10},{10... | collective-permute-start | bytes 1572872 | tf_op jit(solution)/shard_map/ppermute | solution.py:34
  (22 other events, 74.9 us)
